TPU v7x, 32 devices: a whole 2x2x4 slice. The times are simulated.
32 devices in a mesh: axial: 8 (over y, x, core), theta: 4 (over z).
Axes of the slice: x: 2, y: 2, z: 4, core: 2. Of those that a mesh axis runs over, the one named last changes fastest.
Arguments:
- rhs_field: float32 [16, 16, 32, 320], P('theta', 'axial'), may hold values from -6 to 6
- diag_inv: float32 [16, 16, 320, 320], P('theta', 'axial'), may hold values from -0.5 to 2
- lower_block: float32 [16, 16, 320, 320], P('theta', 'axial'), may hold values from -2 to 0.5
- upper_block: float32 [16, 16, 320, 320], P('theta', 'axial'), may hold values from -2 to 0.5
- proj_table: float32 [16, 80, 80], replicated, may hold values from -0.5 to 0.5
- intersection_list: int32 [16, 2], P('theta'), may hold values from 0 to 15
- proj_index: int32 [16, 2], P('theta'), may hold values from 0 to 15
- angle_step: int32 [1], replicated, may hold values from 0 to 15
Outputs:
- solution: float32 [16, 16, 32, 320], P('theta', 'axial')
- mortar: float32 [8, 16, 2560], P('axial', 'theta')
All inputs are finite; a program needn't handle non-finite values.
Results may differ from a plain program's by a relative error of at most 0.0002.
Values sent between devices are 32-bit elements; how exact they have to be, the bound alone decides.
No kernel may reach another device: no remote copies, remote signals or barrier semaphores. Data moves between devices by JAX's collectives and lax.ppermute only.
A program may use at most 64 MiB of HBM per device.

v0:
```python
import jax
import jax.numpy as jnp
from jax import lax
from jax.experimental import pallas as pl
from jax.experimental.pallas import tpu as pltpu
from jax.sharding import PartitionSpec as P


F32 = jnp.float32
BF16 = jnp.bfloat16
PLAIN = (((1,), (0,)), ((), ()))
RIGHT_T = (((1,), (1,)), ((), ()))
BOTH_T = (((0,), (1,)), ((), ()))
VMEM = pl.BlockSpec(memory_space=pltpu.VMEM)
SMEM = pl.BlockSpec(memory_space=pltpu.SMEM)
LIMIT = 12 << 20


def dot(a, b, dims=PLAIN):
    return lax.dot_general(a, b, dims, preferred_element_type=F32)


def split(a):
    high = a.astype(BF16)
    return high, (a - high.astype(F32)).astype(BF16)


def dot3(a, b, dims=PLAIN):
    ah, al = a
    bh, bl = b
    return dot(ah, bh, dims) + (dot(ah, bl, dims) + dot(al, bh, dims))


def rows(vectors, high, low):
    count = vectors.shape[0]
    vh, vl = split(vectors)
    both = dot(jnp.concatenate([vh, vl], axis=0), high)
    return both[:count] + (both[count:] + dot(vh, low))


def call(kernel, out_shape, in_specs, out_specs, flops=0, **kwargs):
    return pl.pallas_call(
        kernel,
        out_shape=out_shape,
        in_specs=in_specs,
        out_specs=out_specs,
        compiler_params=pltpu.CompilerParams(vmem_limit_bytes=LIMIT),
        cost_estimate=pl.CostEstimate(flops=flops, bytes_accessed=0, transcendentals=0),
        **kwargs,
    )


def struct(*shape, dtype=F32):
    return pltpu.VMEM(shape, dtype)


def product_of(left, right, left_stage, right_stage, slot):
    size = left.shape[0]
    high, low = split(left)
    left_stage[slot, :, :size] = high
    left_stage[slot, :, size : 2 * size] = high
    left_stage[slot, :, 2 * size :] = low
    high, low = split(right)
    right_stage[slot, :size] = high
    right_stage[slot, size : 2 * size] = low
    right_stage[slot, 2 * size :] = high
    return -dot(right_stage[slot], left_stage[slot], BOTH_T)


def stages(size):
    return [pltpu.VMEM((2, size, 3 * size), BF16), pltpu.VMEM((2, 3 * size, size), BF16)]


def scaled_rhs(rhs, left_stage, slot):
    high, low = split(rhs)
    return dot(jnp.concatenate([high, low, high], axis=1), left_stage[slot], RIGHT_T)


def first_products(left, right, rhs, flops):
    lines, elems, size, _ = left.shape
    half = lines // 2
    vecs = rhs.shape[2]
    matrix = (half, elems, size, size)
    column = (half, elems, vecs, size)

    def kernel(
        left_hbm, right_hbm, rhs_hbm,
        out_ref, out_g, left_other, left_mine, right_mine, rhs_mine,
        right_other, rhs_other, left_stage, right_stage, sems, rhs_sems,
    ):
        core = core_index()
        mine, other = core * half, (1 - core) * half
        places = [(n, e) for n in range(half) for e in range(elems)]

        def pair(base, left_ref, right_ref, group, n, e):
            index = n * elems + e
            return (
                pltpu.make_async_copy(
                    left_hbm.at[base + n, e], left_ref.at[n, e], sems.at[group, 0, index]
                ),
                pltpu.make_async_copy(
                    right_hbm.at[base + n, e], right_ref.at[n, e], sems.at[group, 1, index]
                ),
            )

        near = [pair(other, left_other, right_other, 0, n, e) for n, e in places]
        far = [pair(mine, left_mine, right_mine, 1, n, e) for n, e in places]
        rhs_near = pltpu.make_async_copy(rhs_hbm.at[pl.ds(other, half)], rhs_other, rhs_sems.at[0])
        rhs_far = pltpu.make_async_copy(rhs_hbm.at[pl.ds(mine, half)], rhs_mine, rhs_sems.at[1])
        for index, copies in enumerate(near):
            for copy in copies:
                copy.start()
            if index == 0:
                rhs_near.start()
        rhs_far.start()
        for index, (n, e) in enumerate(places):
            for copy in near[index]:
                copy.wait()
            for copy in far[index]:
                copy.start()
            if index == 0:
                rhs_near.wait()
            slot = index % 2
            out_ref[n, e] = product_of(
                left_other[n, e], right_other[n, e], left_stage, right_stage, slot
            )
            out_g[n, e] = scaled_rhs(rhs_other[n, e], left_stage, slot)
        for copies in far:
            for copy in copies:
                copy.wait()
        rhs_far.wait()

    hbm = [pltpu.with_memory_space_constraint(x, pltpu.HBM) for x in (left, right, rhs)]
    return call(
        kernel,
        [struct(*shape) for shape in (matrix, column, matrix, matrix, matrix, column)],
        [pl.BlockSpec(memory_space=pltpu.HBM)] * 3,
        [VMEM] * 6,
        flops,
        scratch_shapes=[
            pltpu.VMEM(matrix, F32),
            pltpu.VMEM(column, F32),
            *stages(size),
            pltpu.SemaphoreType.DMA((2, 2, half * elems)),
            pltpu.SemaphoreType.DMA((2,)),
        ],
    )(*hbm)


def second_products(left, right, rhs, later, flops):
    half, elems, size, _ = left.shape

    def kernel(
        left_ref, right_ref, rhs_ref, later_hbm,
        out_ref, out_g, later_other, later_mine, left_stage, right_stage, sems,
    ):
        core = core_index()
        copies = [
            pltpu.make_async_copy(later_hbm.at[pl.ds(base, half)], target, sems.at[index])
            for index, (base, target) in enumerate(
                (((1 - core) * half, later_other), (core * half, later_mine))
            )
        ]
        for copy in copies:
            copy.start()
        for n in range(half):
            for e in range(elems):
                slot = (n * elems + e) % 2
                out_ref[n, e] = product_of(
                    left_ref[n, e], right_ref[n, e], left_stage, right_stage, slot
                )
                out_g[n, e] = scaled_rhs(rhs_ref[n, e], left_stage, slot)
        for copy in copies:
            copy.wait()

    return call(
        kernel,
        [struct(*shape) for shape in (left.shape, rhs.shape, left.shape, left.shape)],
        [VMEM] * 3 + [pl.BlockSpec(memory_space=pltpu.HBM)],
        [VMEM] * 4,
        flops,
        scratch_shapes=[*stages(size), pltpu.SemaphoreType.DMA((2,))],
    )(left, right, rhs, pltpu.with_memory_space_constraint(later, pltpu.HBM))


def late_products(left, right, flops):
    half, elems, size, _ = left.shape

    def kernel(left_ref, right_ref, out_ref, left_stage, right_stage):
        for n in range(half):
            for e in range(elems):
                slot = (n * elems + e) % 2
                out_ref[n, e] = product_of(
                    left_ref[n, e], right_ref[n, e], left_stage, right_stage, slot
                )

    return call(
        kernel, struct(*left.shape), [VMEM] * 2, VMEM, flops, scratch_shapes=stages(size)
    )(left, right)


def composed(high, low, order, flops):
    half, _, size, _ = high.shape

    def kernel(high_ref, low_ref, out_high, out_low, left_stage, right_stage):
        for n in range(half):
            out_high[n, order[0]] = high_ref[n, order[0]]
            out_low[n, order[0]] = low_ref[n, order[0]]
        for before, e in zip(order, order[1:]):
            for n in range(half):
                h, l = out_high[n, before], out_low[n, before]
                left_stage[n, :, :size] = h
                left_stage[n, :, size : 2 * size] = h
                left_stage[n, :, 2 * size :] = l
                right_stage[n, :size] = high_ref[n, e]
                right_stage[n, size : 2 * size] = low_ref[n, e]
                right_stage[n, 2 * size :] = high_ref[n, e]
                h, l = split(dot(left_stage[n], right_stage[n]))
                out_high[n, e] = h
                out_low[n, e] = l

    shape = struct(*high.shape, dtype=BF16)
    return call(
        kernel,
        [shape, shape],
        [VMEM] * 2,
        [VMEM] * 2,
        flops,
        scratch_shapes=[
            pltpu.VMEM((half, size, 3 * size), BF16),
            pltpu.VMEM((half, 3 * size, size), BF16),
        ],
    )(high, low)


def core_index():
    return lax.rem(lax.axis_index("axial"), 2)


def ordered(mine_ref, got_ref, high_ref, low_ref):
    count, elems, _, _ = mine_ref.shape
    core = core_index()
    for source, first in ((mine_ref, core * elems), (got_ref, (1 - core) * elems)):
        for n in range(count):
            for e in range(elems):
                high, low = split(source[n, e])
                high_ref[n, first + e] = high
                low_ref[n, first + e] = low


def local(
    rhs_field,
    diag_inv,
    lower_block,
    upper_block,
    proj_table,
    intersection_list,
    proj_index,
    angle_step,
):
    lines, elems, vecs, size = rhs_field.shape
    devices = lax.axis_size("axial")
    chips = devices // 2
    half = lines // 2
    total = 2 * elems
    partner = [(d, d ^ 1) for d in range(devices)]
    stack = struct(half, total, size, size, dtype=BF16)
    field = struct(half, total, vecs, size)
    edge = struct(half, vecs, size)
    work = half * total * 6 * vecs * size**2

    heavy = half * elems * 6 * size**3
    other_p, other_g, d_other, d_mine, l_mine, r_mine = first_products(
        diag_inv, lower_block, rhs_field, heavy
    )
    got_p = lax.ppermute(other_p, "axial", partner)
    got_g = lax.ppermute(other_g, "axial", partner)
    mine_p, mine_g, u_other, u_mine = second_products(d_mine, l_mine, r_mine, upper_block, heavy)

    def start_kernel(mine_ref, got_ref, mg_ref, gg_ref, high_ref, low_ref, part_ref):
        ordered(mine_ref, got_ref, high_ref, low_ref)
        core = core_index()
        for source, first in ((mg_ref, core * elems), (gg_ref, (1 - core) * elems)):
            for n in range(half):
                for e in range(elems):
                    part_ref[n, first + e] = source[n, e]
        for n in range(half):
            current = part_ref[n, 0]
            for e in range(1, total):
                current = part_ref[n, e] + rows(current, high_ref[n, e], low_ref[n, e])
                part_ref[n, e] = current

    p_high, p_low, parts = call(
        start_kernel, (stack, stack, field), [VMEM] * 4, (VMEM,) * 3, work
    )(mine_p, got_p, mine_g, got_g)
    outgoing = parts[:, -1]

    x_high, x_low = composed(p_high, p_low, list(range(total)), 2 * heavy)

    def hop_kernel(edge_at):
        def kernel(in_ref, high_ref, low_ref, part_ref, out_ref):
            for n in range(half):
                out_ref[n] = part_ref[n, edge_at] + rows(
                    in_ref[n], high_ref[n, edge_at], low_ref[n, edge_at]
                )

        return kernel

    incoming = jnp.zeros_like(outgoing)
    for k in range(chips - 1):
        got = lax.ppermute(outgoing, "axial", [(2 * k + c, 2 * k + 2 + c) for c in range(2)])
        incoming = incoming + got
        if k < chips - 2:
            outgoing = call(hop_kernel(total - 1), edge, [VMEM] * 4, VMEM, work // total)(
                got, x_high, x_low, parts
            )

    other_q = late_products(d_other, u_other, heavy)
    got_q = lax.ppermute(other_q, "axial", partner)
    mine_q = late_products(d_mine, u_mine, heavy)

    q_high, q_low = call(ordered, (stack, stack), [VMEM] * 2, (VMEM,) * 2)(mine_q, got_q)

    def turn_kernel(in_ref, xh_ref, xl_ref, part_ref, qh_ref, ql_ref, back_ref):
        for n in range(half):
            for e in range(total):
                back_ref[n, e] = part_ref[n, e] + rows(in_ref[n], xh_ref[n, e], xl_ref[n, e])
        for n in range(half):
            current = back_ref[n, total - 1]
            for e in reversed(range(total - 1)):
                current = back_ref[n, e] + rows(current, qh_ref[n, e], ql_ref[n, e])
                back_ref[n, e] = current

    backs = call(turn_kernel, field, [VMEM] * 6, VMEM, 2 * work)(
        incoming, x_high, x_low, parts, q_high, q_low
    )
    outgoing = backs[:, 0]

    y_high, y_low = composed(q_high, q_low, list(range(total))[::-1], 2 * heavy)

    incoming = jnp.zeros_like(outgoing)
    for k in reversed(range(1, chips)):
        got = lax.ppermute(outgoing, "axial", [(2 * k + c, 2 * k - 2 + c) for c in range(2)])
        incoming = incoming + got
        if k > 1:
            outgoing = call(hop_kernel(0), edge, [VMEM] * 4, VMEM, work // total)(
                got, y_high, y_low, backs
            )

    def last_kernel(in_ref, high_ref, low_ref, part_ref, mine_ref, other_ref, all_ref):
        for n in range(half):
            for e in range(total):
                all_ref[n, e] = part_ref[n, e] + rows(in_ref[n], high_ref[n, e], low_ref[n, e])
        first = core_index() * elems
        away = (1 - core_index()) * elems
        for n in range(half):
            for e in range(elems):
                mine_ref[n, e] = all_ref[n, first + e]
                other_ref[n, e] = all_ref[n, away + e]

    part = struct(half, elems, vecs, size)
    mine_z, other_z = call(
        last_kernel,
        (part, part),
        [VMEM] * 4,
        (VMEM,) * 2,
        work,
        scratch_shapes=[pltpu.VMEM(field.shape, F32)],
    )(incoming, y_high, y_low, backs)
    got_z = lax.ppermute(other_z, "axial", partner)

    face = proj_table.shape[1]

    def join_kernel(mine_ref, got_ref, field_ref, trace_ref):
        core = core_index()
        for source, base in ((mine_ref, core * half), (got_ref, (1 - core) * half)):
            for n in range(half):
                field_ref[base + n] = source[n]
                trace_ref[base + n] = source[n, elems - 1, :, size - face :]

    solution, traces = call(
        join_kernel,
        (jax.ShapeDtypeStruct(rhs_field.shape, F32), struct(lines, vecs, face)),
        [VMEM] * 2,
        (VMEM,) * 2,
    )(mine_z, got_z)

    groups = lax.axis_size("theta")
    blocks = [traces] + [
        lax.ppermute(traces, "theta", [(t, (t + s) % groups) for t in range(groups)])
        for s in range(1, groups)
    ]
    crossings = intersection_list.shape[1]

    def mortar_kernel(list_ref, index_ref, angle_ref, table_ref, *rest):
        out_ref = rest[-1]
        here = lax.axis_index("theta")
        for g in range(lines):
            sums = jnp.zeros((vecs, face), F32)
            for k in range(crossings):
                face_id = lax.rem(list_ref[g, k] + angle_ref[0], lines * groups)
                shift = lax.rem(here - lax.div(face_id, lines) + groups, groups)
                line = lax.rem(face_id, lines)
                trace = rest[0][line]
                for s in range(1, groups):
                    trace = jnp.where(shift == s, rest[s][line], trace)
                sums = sums + dot3(split(trace), split(table_ref[index_ref[g, k]]), RIGHT_T)
            out_ref[g] = sums

    mortar = call(
        mortar_kernel, jax.ShapeDtypeStruct((lines, vecs, face), F32), [SMEM] * 3 + [VMEM] * (1 + groups), VMEM
    )(intersection_list, proj_index, angle_step, proj_table, *blocks)
    return (solution, mortar.reshape(1, lines, vecs * face))


def solution(mesh):
    block = P("theta", "axial", None, None)
    return jax.shard_map(
        local,
        mesh=mesh,
        in_specs=(block, block, block, block, P(), P("theta", None), P("theta", None), P()),
        out_specs=(block, P("axial", "theta", None)),
        check_vma=False,
    )
```

profile of v0, /device:TPU:0, one launch (start us, length us, event | category | flops | bytes accessed | tf_op | source)
XLA Modules:
  0.0 72.8 jit_solution(18036969736932150008)
XLA Ops:
  0.6 5.7 %shard_map.95 = (f32[2,2,320,320]{3,2,1,0:T(8,128)S(1)}, f32[2,2,32,320]{3,2,1,0:T(8,128)S(1)}, f32[2,2,320,320]{3,2,1,0:T(8,128)S(1)}, f32[2,2,320,320]{3,2,1,0...) custom-call(f32[4,2,320,320]{3,2,1,0:T(8,128)} %left_hbm.1, f32[4,2,320,320]{3,2,1,0:T(8,128)} %right_hbm.1, ...), custom_call_target="tpu_custom_call" | custom-call | flops 786432000 | tf_op jit(solution)/shard_map/pallas_call | solution.py:134
  6.4 0.6 collective-permute-start
  6.9 4.6 %shard_map.96 = (f32[2,2,320,320]{3,2,1,0:T(8,128)S(1)}, f32[2,2,32,320]{3,2,1,0:T(8,128)S(1)}, f32[2,2,320,320]{3,2,1,0:T(8,128)S(1)}, f32[2,2,320,320]{3,2,1,0:T(8,128)S(1)}) custom-call(f32[2,2,320,320]{3,2,1,0:T(8,128)S(1)} %get-tuple-element.25.left_ref, f32[2,2,320,320]{3,2,1,0:T(8,128)S(1)} %get-tuple-element.26.right_ref, ...), custom_call_target="tpu_custom_call" | custom-call | flops 786432000 | tf_op jit(solution)/shard_map/pallas_call | solution.py:176
  11.5 2.0 %shard_map.102 = f32[2,2,320,320]{3,2,1,0:T(8,128)S(1)} custom-call(f32[2,2,320,320]{3,2,1,0:T(8,128)S(1)} %get-tuple-element.38.left_ref, f32[2,2,320,320]{3,2,1,0:T(8,128)S(1)} %get-tuple-element.39.right_ref), custom_call_target="tpu_custom_call" | custom-call | flops 786432000 | tf_op jit(solution)/shard_map/pallas_call | solution.py:197
  13.5 0.1 collective-permute-start.5
  13.6 0.5 collective-permute-start.1
  14.1 3.7 %collective-permute-done.1.gg_ref = f32[2,2,32,320]{3,2,1,0:T(8,128)S(1)} collective-permute-done((f32[2,2,32,320]{3,2,1,0:T(8,128)S(1)}, f32[2,2,32,320]{3,2,1,0:T(8,128)S(1)}, u32[]{:S(2)}, u32[]{:S(2)}) %collective-permute-start.1) | collective-permute-done | bytes 163872 | tf_op jit(solution)/shard_map/ppermute | solution.py:277
  17.8 0.0 collective-permute-done.got_ref
  17.8 1.7 %shard_map.97 = (bf16[2,4,320,320]{3,2,1,0:T(8,128)(2,1)S(1)}, bf16[2,4,320,320]{3,2,1,0:T(8,128)(2,1)S(1)}, f32[2,4,32,320]{3,2,1,0:T(8,128)S(1)}) custom-call(f32[2,2,320,320]{3,2,1,0:T(8,128)S(1)} %get-tuple-element.28.mine_ref, f32[2,2,320,320]{3,2,1,0:T(8,128)S(1)} %collective-permute-done.got_ref, f32[2,2,32,320]{3,2,1,0:T(8,128)S(1)} %get-tuple-element.30.mg_ref, ...), custom_call_target="tpu_custom_call" | custom-call | flops 157286400 | tf_op jit(solution)/shard_map/pallas_call | solution.py:293
  19.5 4.5 %collective-permute-start.2 = (f32[2,32,320]{2,1,0:T(8,128)S(1)}, f32[2,32,320]{2,1,0:T(8,128)S(1)}, u32[]{:S(2)}, u32[]{:S(2)}) collective-permute-start(f32[2,32,320]{2,1,0:T(8,128)S(1)} %slice_bitcast_fusion.1), channel_id=1, source_target_pairs={{0,8},{4,12},{1,9},{5,13},{2,10},{6,14},{3,11},{7,15}} | collective-permute-start | bytes 245768 | tf_op jit(solution)/shard_map/ppermute | solution.py:311
  24.0 2.6 %shard_map.98 = (bf16[2,4,320,320]{3,2,1,0:T(8,128)(2,1)S(1)}, bf16[2,4,320,320]{3,2,1,0:T(8,128)(2,1)S(1)}) custom-call(bf16[2,4,320,320]{3,2,1,0:T(8,128)(2,1)S(1)} %get-tuple-element.33.high_ref, bf16[2,4,320,320]{3,2,1,0:T(8,128)(2,1)S(1)} %get-tuple-element.34.low_ref), custom_call_target="tpu_custom_call" | custom-call | flops 1572864000 | tf_op jit(solution)/shard_map/pallas_call | solution.py:223
  26.7 0.0 collective-permute-done.2.in_ref
  26.7 0.3 shard_map.99
  27.0 0.7 collective-permute-start.3
  27.7 0.0 collective-permute-done.3.in_ref
  27.7 0.3 shard_map.100
  28.0 0.8 %collective-permute-start.4 = (f32[2,32,320]{2,1,0:T(8,128)S(1)}, f32[2,32,320]{2,1,0:T(8,128)S(1)}, u32[]{:S(2)}, u32[]{:S(2)}) collective-permute-start(f32[2,32,320]{2,1,0:T(8,128)S(1)} %shard_map.100), channel_id=1, source_target_pairs={{16,24},{20,28},{17,25},{21,29},{18,26},{22,30},{19,27},{23,31}} | collective-permute-start | bytes 245768 | tf_op jit(solution)/shard_map/ppermute | solution.py:311
  28.8 2.0 %shard_map.101.mine_ref = f32[2,2,320,320]{3,2,1,0:T(8,128)S(1)} custom-call(f32[2,2,320,320]{3,2,1,0:T(8,128)S(1)} %get-tuple-element.25.left_ref, f32[2,2,320,320]{3,2,1,0:T(8,128)S(1)} %get-tuple-element.37.right_ref), custom_call_target="tpu_custom_call" | custom-call | flops 786432000 | tf_op jit(solution)/shard_map/pallas_call | solution.py:197
  30.8 0.0 collective-permute-done.5.got_ref
  30.8 0.8 %shard_map.103 = (bf16[2,4,320,320]{3,2,1,0:T(8,128)(2,1)S(1)}, bf16[2,4,320,320]{3,2,1,0:T(8,128)(2,1)S(1)}) custom-call(f32[2,2,320,320]{3,2,1,0:T(8,128)S(1)} %shard_map.101.mine_ref, f32[2,2,320,320]{3,2,1,0:T(8,128)S(1)} %collective-permute-done.5.got_ref), custom_call_target="tpu_custom_call" | custom-call | tf_op jit(solution)/shard_map/pallas_call | solution.py:322
  31.6 0.0 collective-permute-done.4
  31.6 1.8 %shard_map.104.part_ref = f32[2,4,32,320]{3,2,1,0:T(8,128)S(1)} custom-call(f32[2,32,320]{2,1,0:T(8,128)S(1)} %add_add_fusion.1.in_ref, bf16[2,4,320,320]{3,2,1,0:T(8,128)(2,1)S(1)} %get-tuple-element.35.high_ref.xh_ref, bf16[2,4,320,320]{3,2,1,0:T(8,128)(2,1)S(1)} %get-tuple-element.36.low_ref.xl_ref, f32[2,4,32,320]{3,2,1,0:T(8,128)S(1)} %get-tuple-element.32.part_ref, ...), custom_call_target="tpu_custom_call" | custom-call | flops 314572800 | tf_op jit(solution)/shard_map/pallas_call | solution.py:334
  33.4 0.7 collective-permute-start.6
  34.1 2.6 %shard_map.105 = (bf16[2,4,320,320]{3,2,1,0:T(8,128)(2,1)S(1)}, bf16[2,4,320,320]{3,2,1,0:T(8,128)(2,1)S(1)}) custom-call(bf16[2,4,320,320]{3,2,1,0:T(8,128)(2,1)S(1)} %get-tuple-element.40.qh_ref.high_ref, bf16[2,4,320,320]{3,2,1,0:T(8,128)(2,1)S(1)} %get-tuple-element.41.ql_ref.low_ref), custom_call_target="tpu_custom_call" | custom-call | flops 1572864000 | tf_op jit(solution)/shard_map/pallas_call | solution.py:223
  36.8 0.0 collective-permute-done.6.in_ref
  36.8 0.3 shard_map.106
  37.1 0.7 collective-permute-start.7
  37.8 0.0 collective-permute-done.7.in_ref
  37.8 0.3 shard_map.107
  38.1 1.3 %collective-permute-start.8 = (f32[2,32,320]{2,1,0:T(8,128)S(1)}, f32[2,32,320]{2,1,0:T(8,128)S(1)}, u32[]{:S(2)}, u32[]{:S(2)}) collective-permute-start(f32[2,32,320]{2,1,0:T(8,128)S(1)} %shard_map.107), channel_id=1, source_target_pairs={{8,0},{12,4},{9,1},{13,5},{10,2},{14,6},{11,3},{15,7}} | collective-permute-start | bytes 245768 | tf_op jit(solution)/shard_map/ppermute | solution.py:343
  39.4 18.1 %collective-permute-done.8 = f32[2,32,320]{2,1,0:T(8,128)S(1)} collective-permute-done((f32[2,32,320]{2,1,0:T(8,128)S(1)}, f32[2,32,320]{2,1,0:T(8,128)S(1)}, u32[]{:S(2)}, u32[]{:S(2)}) %collective-permute-start.8) | collective-permute-done | bytes 81952 | tf_op jit(solution)/shard_map/ppermute | solution.py:343
  57.5 0.0 copy-start.1
  57.5 0.0 copy-start.2
  57.5 0.0 copy-start
  57.5 0.9 %shard_map.108 = (f32[2,2,32,320]{3,2,1,0:T(8,128)S(1)}, f32[2,2,32,320]{3,2,1,0:T(8,128)S(1)}) custom-call(f32[2,32,320]{2,1,0:T(8,128)S(1)} %add_add_fusion.in_ref, bf16[2,4,320,320]{3,2,1,0:T(8,128)(2,1)S(1)} %get-tuple-element.42.high_ref, bf16[2,4,320,320]{3,2,1,0:T(8,128)(2,1)S(1)} %get-tuple-element.43.low_ref, f32[2,4,32,320]{3,2,1,0:T(8,128)S(1)} %shard_map.104.part_ref), custom_call_target="tpu_custom_call" | custom-call | flops 157286400 | tf_op jit(solution)/shard_map/pallas_call | solution.py:362
  58.4 0.1 collective-permute-start.9
  58.5 1.4 %collective-permute-done.9.got_ref = f32[2,2,32,320]{3,2,1,0:T(8,128)S(1)} collective-permute-done((f32[2,2,32,320]{3,2,1,0:T(8,128)S(1)}, f32[2,2,32,320]{3,2,1,0:T(8,128)S(1)}, u32[]{:S(2)}, u32[]{:S(2)}) %collective-permute-start.9) | collective-permute-done | bytes 163872 | tf_op jit(solution)/shard_map/ppermute | solution.py:370
  59.9 0.8 %shard_map.109 = (f32[4,2,32,320]{3,2,1,0:T(8,128)}, f32[4,32,80]{2,1,0:T(8,128)S(1)}) custom-call(f32[2,2,32,320]{3,2,1,0:T(8,128)S(1)} %get-tuple-element.44.mine_ref, f32[2,2,32,320]{3,2,1,0:T(8,128)S(1)} %collective-permute-done.9.got_ref), custom_call_target="tpu_custom_call" | custom-call | tf_op jit(solution)/shard_map/pallas_call | solution.py:381
  60.7 3.6 %collective-permute-start.12 = (f32[4,32,80]{2,1,0:T(8,128)S(1)}, f32[4,32,80]{2,1,0:T(8,128)S(1)}, u32[]{:S(2)}, u32[]{:S(2)}) collective-permute-start(f32[4,32,80]{2,1,0:T(8,128)S(1)} %get-tuple-element.47.rest_0_), channel_id=1, source_target_pairs={{0,3},{1,0},{2,1},{3,2},{4,7},{5,4},{6,5},{7,6},{8,11},{9,8},{10,9... | collective-permute-start | bytes 122888 | tf_op jit(solution)/shard_map/ppermute | solution.py:390
  64.3 0.0 collective-permute-start.11
  64.3 1.0 %collective-permute-start.10 = (f32[4,32,80]{2,1,0:T(8,128)S(1)}, f32[4,32,80]{2,1,0:T(8,128)S(1)}, u32[]{:S(2)}, u32[]{:S(2)}) collective-permute-start(f32[4,32,80]{2,1,0:T(8,128)S(1)} %get-tuple-element.47.rest_0_), channel_id=1, source_target_pairs={{0,1},{1,2},{2,3},{3,0},{4,5},{5,6},{6,7},{7,4},{8,9},{9,10},{10,1... | collective-permute-start | bytes 122888 | tf_op jit(solution)/shard_map/ppermute | solution.py:390
  66.0 0.1 copy.12.list_ref
  66.1 0.1 copy.13.index_ref
  66.2 0.6 collective-permute-done.12.rest_3_
  66.8 4.3 %collective-permute-done.11.rest_2_ = f32[4,32,80]{2,1,0:T(8,128)S(1)} collective-permute-done((f32[4,32,80]{2,1,0:T(8,128)S(1)}, f32[4,32,80]{2,1,0:T(8,128)S(1)}, u32[]{:S(2)}, u32[]{:S(2)}) %collective-permute-start.11) | collective-permute-done | bytes 40992 | tf_op jit(solution)/shard_map/ppermute | solution.py:390
  71.1 0.0 collective-permute-done.10.rest_1_
  71.1 1.0 %shard_map.110 = f32[4,32,80]{2,1,0:T(8,128)S(1)} custom-call(s32[4,2]{1,0:T(4,128)S(1)} %copy.12.list_ref, s32[4,2]{1,0:T(4,128)S(1)} %copy.13.index_ref, s32[1]{0:T(128)S(6)} %copy.17.angle_ref, f32[16,80,80]{2,1,0:T(8,128)S(1)} %copy-done, f32[4,32,80]{2,1,0:T(8,128)S(1)} %get-tuple-element.47.rest_0_, f32[4,32,80]{2,1,0:T(8,128)S(1)} %collective-permute-done.10.rest_1_, ...), custom_call_target="tpu_custom_call" | custom-call | tf_op jit(solution)/shard_map/pallas_call | solution.py:410
  72.0 0.7 %reshape.7 = f32[1,4,2560]{2,1,0:T(4,128)} reshape(f32[4,32,80]{2,1,0:T(8,128)S(1)} %shard_map.110) | data formatting | bytes 81920 | tf_op jit(solution)/shard_map/reshape | solution.py:413
  (7 shorter events, 0.1 us)
Async XLA Ops:
  6.4 11.5 %collective-permute-start = (f32[2,2,320,320]{3,2,1,0:T(8,128)S(1)}, f32[2,2,320,320]{3,2,1,0:T(8,128)S(1)}, u32[]{:S(2)}, u32[]{:S(2)}) collective-permute-start(f32[2,2,320,320]{3,2,1,0:T(8,128)S(1)} %get-tuple-element.29), channel_id=1, source_target_pairs={{0,4},{4,0},{8,12},{12,8},{16,20},{20,16},{24,28},{28,24},{1,5},{5... | collective-permute-start | bytes 4915208 | tf_op jit(solution)/shard_map/ppermute | solution.py:276
  13.5 17.3 %collective-permute-start.5 = (f32[2,2,320,320]{3,2,1,0:T(8,128)S(1)}, f32[2,2,320,320]{3,2,1,0:T(8,128)S(1)}, u32[]{:S(2)}, u32[]{:S(2)}) collective-permute-start(f32[2,2,320,320]{3,2,1,0:T(8,128)S(1)} %shard_map.102), channel_id=1, source_target_pairs={{0,4},{4,0},{8,12},{12,8},{16,20},{20,16},{24,28},{28,24},{1,5},{5... | collective-permute-start | bytes 4915208 | tf_op jit(solution)/shard_map/ppermute | solution.py:319
  13.6 4.2 %collective-permute-start.1 = (f32[2,2,32,320]{3,2,1,0:T(8,128)S(1)}, f32[2,2,32,320]{3,2,1,0:T(8,128)S(1)}, u32[]{:S(2)}, u32[]{:S(2)}) collective-permute-start(f32[2,2,32,320]{3,2,1,0:T(8,128)S(1)} %get-tuple-element.31), channel_id=1, source_target_pairs={{0,4},{4,0},{8,12},{12,8},{16,20},{20,16},{24,28},{28,24},{1,5},{5... | collective-permute-start | bytes 491528 | tf_op jit(solution)/shard_map/ppermute | solution.py:277
  19.5 7.2 %collective-permute-start.2 = (f32[2,32,320]{2,1,0:T(8,128)S(1)}, f32[2,32,320]{2,1,0:T(8,128)S(1)}, u32[]{:S(2)}, u32[]{:S(2)}) collective-permute-start(f32[2,32,320]{2,1,0:T(8,128)S(1)} %slice_bitcast_fusion.1), channel_id=1, source_target_pairs={{0,8},{4,12},{1,9},{5,13},{2,10},{6,14},{3,11},{7,15}} | collective-permute-start | bytes 245768 | tf_op jit(solution)/shard_map/ppermute | solution.py:311
  27.0 0.7 collective-permute-start.3
  28.0 3.6 %collective-permute-start.4 = (f32[2,32,320]{2,1,0:T(8,128)S(1)}, f32[2,32,320]{2,1,0:T(8,128)S(1)}, u32[]{:S(2)}, u32[]{:S(2)}) collective-permute-start(f32[2,32,320]{2,1,0:T(8,128)S(1)} %shard_map.100), channel_id=1, source_target_pairs={{16,24},{20,28},{17,25},{21,29},{18,26},{22,30},{19,27},{23,31}} | collective-permute-start | bytes 245768 | tf_op jit(solution)/shard_map/ppermute | solution.py:311
  33.4 3.3 %collective-permute-start.6 = (f32[2,32,320]{2,1,0:T(8,128)S(1)}, f32[2,32,320]{2,1,0:T(8,128)S(1)}, u32[]{:S(2)}, u32[]{:S(2)}) collective-permute-start(f32[2,32,320]{2,1,0:T(8,128)S(1)} %slice_bitcast_fusion), channel_id=1, source_target_pairs={{24,16},{28,20},{25,17},{29,21},{26,18},{30,22},{27,19},{31,23}} | collective-permute-start | bytes 245768 | tf_op jit(solution)/shard_map/ppermute | solution.py:343
  37.1 0.7 collective-permute-start.7
  38.1 19.4 %collective-permute-start.8 = (f32[2,32,320]{2,1,0:T(8,128)S(1)}, f32[2,32,320]{2,1,0:T(8,128)S(1)}, u32[]{:S(2)}, u32[]{:S(2)}) collective-permute-start(f32[2,32,320]{2,1,0:T(8,128)S(1)} %shard_map.107), channel_id=1, source_target_pairs={{8,0},{12,4},{9,1},{13,5},{10,2},{14,6},{11,3},{15,7}} | collective-permute-start | bytes 245768 | tf_op jit(solution)/shard_map/ppermute | solution.py:343
  57.5 8.5 %copy-start.1 = (s32[4,2]{0,1:T(2,128)S(1)}, s32[4,2]{0,1:T(2,128)}, u32[]{:S(2)}) copy-start(s32[4,2]{0,1:T(2,128)} %param.13) | copy-start | bytes 100
  57.5 8.6 %copy-start.2 = (s32[4,2]{0,1:T(2,128)S(1)}, s32[4,2]{0,1:T(2,128)}, u32[]{:S(2)}) copy-start(s32[4,2]{0,1:T(2,128)} %param.14) | copy-start | bytes 100
  57.5 13.6 %copy-start = (f32[16,80,80]{2,1,0:T(8,128)S(1)}, f32[16,80,80]{2,1,0:T(8,128)}, u32[]{:S(2)}) copy-start(f32[16,80,80]{2,1,0:T(8,128)} %table_ref.1) | copy-start | bytes 1228804
  58.4 1.5 %collective-permute-start.9 = (f32[2,2,32,320]{3,2,1,0:T(8,128)S(1)}, f32[2,2,32,320]{3,2,1,0:T(8,128)S(1)}, u32[]{:S(2)}, u32[]{:S(2)}) collective-permute-start(f32[2,2,32,320]{3,2,1,0:T(8,128)S(1)} %get-tuple-element.45), channel_id=1, source_target_pairs={{0,4},{4,0},{8,12},{12,8},{16,20},{20,16},{24,28},{28,24},{1,5},{5... | collective-permute-start | bytes 491528 | tf_op jit(solution)/shard_map/ppermute | solution.py:370
  60.7 6.1 %collective-permute-start.12 = (f32[4,32,80]{2,1,0:T(8,128)S(1)}, f32[4,32,80]{2,1,0:T(8,128)S(1)}, u32[]{:S(2)}, u32[]{:S(2)}) collective-permute-start(f32[4,32,80]{2,1,0:T(8,128)S(1)} %get-tuple-element.47.rest_0_), channel_id=1, source_target_pairs={{0,3},{1,0},{2,1},{3,2},{4,7},{5,4},{6,5},{7,6},{8,11},{9,8},{10,9... | collective-permute-start | bytes 122888 | tf_op jit(solution)/shard_map/ppermute | solution.py:390
  64.3 6.8 %collective-permute-start.11 = (f32[4,32,80]{2,1,0:T(8,128)S(1)}, f32[4,32,80]{2,1,0:T(8,128)S(1)}, u32[]{:S(2)}, u32[]{:S(2)}) collective-permute-start(f32[4,32,80]{2,1,0:T(8,128)S(1)} %get-tuple-element.47.rest_0_), channel_id=1, source_target_pairs={{0,2},{1,3},{2,0},{3,1},{4,6},{5,7},{6,4},{7,5},{8,10},{9,11},{10,... | collective-permute-start | bytes 122888 | tf_op jit(solution)/shard_map/ppermute | solution.py:390
  64.3 6.8 %collective-permute-start.10 = (f32[4,32,80]{2,1,0:T(8,128)S(1)}, f32[4,32,80]{2,1,0:T(8,128)S(1)}, u32[]{:S(2)}, u32[]{:S(2)}) collective-permute-start(f32[4,32,80]{2,1,0:T(8,128)S(1)} %get-tuple-element.47.rest_0_), channel_id=1, source_target_pairs={{0,1},{1,2},{2,3},{3,0},{4,5},{5,6},{6,7},{7,4},{8,9},{9,10},{10,1... | collective-permute-start | bytes 122888 | tf_op jit(solution)/shard_map/ppermute | solution.py:390
where the time goes:
time: 73 us; the launch traced here: 72.8 us
  waiting for transfers between devices  28.2 us (39%)
  Pallas kernels  27.6 us (38%)
  starting transfers between devices  14.5 us (20%)
  between operations  1.53 us (2%)
  local copies, waits for them, and re-layouts  0.97 us (1%)
    ppermute x3, waiting for transfers between devices, local(): lax.ppermute(outgoing, 'axial', [(2 * k + c, 2 * k - 2 + c) for c in rang...  18.1 us
    ppermute x3, starting transfers between devices, local(): lax.ppermute(outgoing, 'axial', [(2 * k + c, 2 * k + 2 + c) for c in rang...  6.04 us
    pallas_call x1, Pallas kernels, first_products(): call(kernel, [struct(*shape) for shape in (matrix, column, matrix, matrix...  5.71 us
    pallas_call x2, Pallas kernels, composed(): call(kernel, [shape, shape], [VMEM] * 2, [VMEM] * 2, flops, scratch_shape...  5.27 us
    ppermute x3, waiting for transfers between devices, local(): lax.ppermute(traces, 'theta', [(t, (t + s) % groups) for t in range(group...  4.91 us
    ppermute x3, starting transfers between devices, local(): lax.ppermute(traces, 'theta', [(t, (t + s) % groups) for t in range(group...  4.62 us
    pallas_call x1, Pallas kernels, second_products(): call(kernel, [struct(*shape) for shape in (left.shape, rhs.shape, left.sh...  4.61 us
    pallas_call x2, Pallas kernels, late_products(): call(kernel, struct(*left.shape), [VMEM] * 2, VMEM, flops, scratch_shapes...  3.92 us
  transfers between devices with their start and end apart: 13, of which 5 were waited for; matrix products, arithmetic and copies ran while one was open for 0% of the time, Pallas kernels for 23%

commit v1 on v0

v1 whole, which is shorter than its diff:
```python
import jax
import jax.numpy as jnp
from jax import lax
from jax.experimental import pallas as pl
from jax.experimental.pallas import tpu as pltpu
from jax.sharding import PartitionSpec as P


F32 = jnp.float32
BF16 = jnp.bfloat16
PLAIN = (((1,), (0,)), ((), ()))
RIGHT_T = (((1,), (1,)), ((), ()))
BOTH_T = (((0,), (1,)), ((), ()))
VMEM = pl.BlockSpec(memory_space=pltpu.VMEM)
SMEM = pl.BlockSpec(memory_space=pltpu.SMEM)
LIMIT = 12 << 20


def dot(a, b, dims=PLAIN):
    return lax.dot_general(a, b, dims, preferred_element_type=F32)


def split(a):
    high = a.astype(BF16)
    return high, (a - high.astype(F32)).astype(BF16)


def dot3(a, b, dims=PLAIN):
    ah, al = a
    bh, bl = b
    return dot(ah, bh, dims) + (dot(ah, bl, dims) + dot(al, bh, dims))


def rows(vectors, high, low):
    count = vectors.shape[0]
    vh, vl = split(vectors)
    both = dot(jnp.concatenate([vh, vl], axis=0), high)
    return both[:count] + (both[count:] + dot(vh, low))


def call(kernel, out_shape, in_specs, out_specs, flops=0, **kwargs):
    return pl.pallas_call(
        kernel,
        out_shape=out_shape,
        in_specs=in_specs,
        out_specs=out_specs,
        compiler_params=pltpu.CompilerParams(vmem_limit_bytes=LIMIT),
        cost_estimate=pl.CostEstimate(flops=flops, bytes_accessed=0, transcendentals=0),
        **kwargs,
    )


def struct(*shape, dtype=F32):
    return pltpu.VMEM(shape, dtype)


def product_of(left, right, left_stage, right_stage, slot):
    size, width = right.shape
    high, low = split(left)
    left_stage[slot, :, :size] = high
    left_stage[slot, :, size : 2 * size] = high
    left_stage[slot, :, 2 * size :] = low
    high, low = split(right)
    right_stage[slot, :size, :width] = high
    right_stage[slot, size : 2 * size, :width] = low
    right_stage[slot, 2 * size :, :width] = high
    return dot(right_stage[slot, :, :width], left_stage[slot], BOTH_T)


def stages(size, width):
    return [pltpu.VMEM((2, size, 3 * size), BF16), pltpu.VMEM((2, 3 * size, width), BF16)]


def products(left_ref, right_ref, rhs_ref, out_ref, out_g, left_stage, right_stage):
    half, elems, _, _ = left_ref.shape
    for n in range(half):
        for e in range(elems):
            slot = (n * elems + e) % 2
            out_ref[n, e] = -product_of(
                left_ref[n, e], right_ref[n, e], left_stage, right_stage, slot
            )
            high, low = split(rhs_ref[n, e])
            terms = jnp.concatenate([high, low, high], axis=1)
            out_g[n, e] = dot(terms, left_stage[slot], RIGHT_T)


def first_products(left, right, rhs, flops):
    lines, elems, size, _ = left.shape
    half = lines // 2
    vecs = rhs.shape[2]
    matrix = (half, elems, size, size)
    column = (half, elems, vecs, size)

    def kernel(
        left_hbm, right_hbm, rhs_hbm,
        out_ref, out_g, left_other, left_mine, right_mine, rhs_mine,
        right_other, rhs_other, left_stage, right_stage, sems,
    ):
        core = core_index()
        targets = ((left_other, right_other, rhs_other), (left_mine, right_mine, rhs_mine))
        near, far = (
            [
                pltpu.make_async_copy(
                    source.at[pl.ds(base * half, half)], target, sems.at[group, i]
                )
                for i, (source, target) in enumerate(zip((left_hbm, right_hbm, rhs_hbm), refs))
            ]
            for group, (base, refs) in enumerate(zip((1 - core, core), targets))
        )
        for copy in near + far:
            copy.start()
        for copy in near:
            copy.wait()
        products(left_other, right_other, rhs_other, out_ref, out_g, left_stage, right_stage)
        for copy in far:
            copy.wait()

    hbm = [pltpu.with_memory_space_constraint(x, pltpu.HBM) for x in (left, right, rhs)]
    return call(
        kernel,
        [struct(*shape) for shape in (matrix, column, matrix, matrix, matrix, column)],
        [pl.BlockSpec(memory_space=pltpu.HBM)] * 3,
        [VMEM] * 6,
        flops,
        scratch_shapes=[
            pltpu.VMEM(matrix, F32),
            pltpu.VMEM(column, F32),
            *stages(size, size),
            pltpu.SemaphoreType.DMA((2, 3)),
        ],
    )(*hbm)


def second_products(left, right, rhs, flops):
    size = left.shape[2]
    return call(
        products,
        [struct(*left.shape), struct(*rhs.shape)],
        [VMEM] * 3,
        [VMEM] * 2,
        flops,
        scratch_shapes=stages(size, size),
    )(left, right, rhs)


def late_products(left, right, flops):
    half, elems, size, _ = left.shape

    def kernel(left_ref, right_ref, out_ref, left_stage, right_stage):
        for n in range(half):
            for e in range(elems):
                slot = (n * elems + e) % 2
                out_ref[n, e] = -product_of(
                    left_ref[n, e], right_ref[n, e], left_stage, right_stage, slot
                )

    return call(
        kernel, struct(*left.shape), [VMEM] * 2, VMEM, flops, scratch_shapes=stages(size, size)
    )(left, right)


def stage_left(stage, n, start, count, high, low):
    size = high.shape[1]
    stage[n, start : start + count, :size] = high
    stage[n, start : start + count, size : 2 * size] = high
    stage[n, start : start + count, 2 * size :] = low


def stage_right(stage, n, high, low):
    size = high.shape[0]
    stage[n, :size] = high
    stage[n, size : 2 * size] = low
    stage[n, 2 * size :] = high


def composed(mine, got, order, flops, later=None):
    half, elems, size, _ = mine.shape

    def kernel(mine_ref, got_ref, *rest):
        copies = []
        if later is not None:
            later_hbm, *rest, sems = rest
            targets = rest[2:4]
            core = core_index()
            copies = [
                pltpu.make_async_copy(later_hbm.at[pl.ds(base * half, half)], target, sems.at[i])
                for i, (base, target) in enumerate(zip((1 - core, core), targets))
            ]
        out_high, out_low, *_, left_stage, right_stage = rest
        for copy in copies:
            copy.start()
        for n in range(half):
            first = pick(mine_ref, got_ref, n, order[0])
            out_high[n, order[0]], out_low[n, order[0]] = split(first)
        for before, e in zip(order, order[1:]):
            for n in range(half):
                stage_left(left_stage, n, 0, size, out_high[n, before], out_low[n, before])
                stage_right(right_stage, n, *split(pick(mine_ref, got_ref, n, e)))
                out_high[n, e], out_low[n, e] = split(dot(left_stage[n], right_stage[n]))
        for copy in copies:
            copy.wait()

    shapes = [struct(half, len(order), size, size, dtype=BF16)] * 2
    specs, operands = [VMEM] * 2, [mine, got]
    scratch = [
        pltpu.VMEM((half, size, 3 * size), BF16),
        pltpu.VMEM((half, 3 * size, size), BF16),
    ]
    if later is not None:
        shapes += [struct(half, elems, size, size)] * 2
        specs.append(pl.BlockSpec(memory_space=pltpu.HBM))
        operands.append(pltpu.with_memory_space_constraint(later, pltpu.HBM))
        scratch.append(pltpu.SemaphoreType.DMA((2,)))
    return call(
        kernel, shapes, specs, [VMEM] * len(shapes), flops, scratch_shapes=scratch
    )(*operands)


def turned(x_high, x_low, parts, mine, got, flops):
    half, total, size, _ = x_high.shape
    vecs = parts.shape[2]

    def kernel(
        xh_ref, xl_ref, part_ref, mine_ref, got_ref,
        out_high, out_low, out_part, left_stage, right_stage,
    ):
        last = total - 1
        for n in range(half):
            out_high[n, last] = xh_ref[n, last]
            out_low[n, last] = xl_ref[n, last]
            out_part[n, last] = part_ref[n, last]
        for e in reversed(range(last)):
            for n in range(half):
                stage_left(left_stage, n, 0, size, out_high[n, e + 1], out_low[n, e + 1])
                stage_left(left_stage, n, size, vecs, *split(out_part[n, e + 1]))
                stage_right(right_stage, n, *split(pick(mine_ref, got_ref, n, e)))
                result = dot(left_stage[n], right_stage[n])
                x = xh_ref[n, e].astype(F32) + xl_ref[n, e].astype(F32)
                out_high[n, e], out_low[n, e] = split(x + result[:size])
                out_part[n, e] = part_ref[n, e] + result[size:]

    shape = struct(*x_high.shape, dtype=BF16)
    return call(
        kernel,
        [shape, shape, struct(*parts.shape)],
        [VMEM] * 5,
        [VMEM] * 3,
        flops,
        scratch_shapes=[
            pltpu.VMEM((half, size + vecs, 3 * size), BF16),
            pltpu.VMEM((half, 3 * size, size), BF16),
        ],
    )(x_high, x_low, parts, mine, got)


def core_index():
    return lax.rem(lax.axis_index("axial"), 2)


def pick(mine_ref, got_ref, n, e):
    elems = mine_ref.shape[1]
    owner, place = divmod(e, elems)
    return jnp.where(core_index() == owner, mine_ref[n, place], got_ref[n, place])


def local(
    rhs_field,
    diag_inv,
    lower_block,
    upper_block,
    proj_table,
    intersection_list,
    proj_index,
    angle_step,
):
    lines, elems, vecs, size = rhs_field.shape
    devices = lax.axis_size("axial")
    chips = devices // 2
    half = lines // 2
    total = 2 * elems
    partner = [(d, d ^ 1) for d in range(devices)]
    field = struct(half, total, vecs, size)
    edge = struct(half, vecs, size)
    work = half * total * 6 * vecs * size**2

    heavy = half * elems * 6 * size**3
    other_p, other_g, d_other, d_mine, l_mine, r_mine = first_products(
        diag_inv, lower_block, rhs_field, heavy
    )
    got_p = lax.ppermute(other_p, "axial", partner)
    got_g = lax.ppermute(other_g, "axial", partner)
    mine_p, mine_g = second_products(d_mine, l_mine, r_mine, heavy)

    def start_kernel(mine_ref, got_ref, mine_g_ref, got_g_ref, part_ref):
        for n in range(half):
            current = pick(mine_g_ref, got_g_ref, n, 0)
            part_ref[n, 0] = current
            for e in range(1, total):
                operator = split(pick(mine_ref, got_ref, n, e))
                current = pick(mine_g_ref, got_g_ref, n, e) + rows(current, *operator)
                part_ref[n, e] = current

    parts = call(start_kernel, field, [VMEM] * 4, VMEM, work)(mine_p, got_p, mine_g, got_g)
    outgoing = parts[:, -1]

    x_high, x_low, u_other, u_mine = composed(
        mine_p, got_p, list(range(total)), 2 * heavy, upper_block
    )

    def hop_kernel(edge_at):
        def kernel(in_ref, high_ref, low_ref, part_ref, out_ref):
            for n in range(half):
                out_ref[n] = part_ref[n, edge_at] + rows(
                    in_ref[n], high_ref[n, edge_at], low_ref[n, edge_at]
                )

        return kernel

    incoming = jnp.zeros_like(outgoing)
    for k in range(chips - 1):
        got = lax.ppermute(outgoing, "axial", [(2 * k + c, 2 * k + 2 + c) for c in range(2)])
        incoming = incoming + got
        if k < chips - 2:
            outgoing = call(hop_kernel(total - 1), edge, [VMEM] * 4, VMEM, work // total)(
                got, x_high, x_low, parts
            )

    other_q = late_products(d_other, u_other, heavy)
    got_q = lax.ppermute(other_q, "axial", partner)
    mine_q = late_products(d_mine, u_mine, heavy)

    t_high, t_low, t_parts = turned(x_high, x_low, parts, mine_q, got_q, 2 * heavy)

    outgoing = call(hop_kernel(0), edge, [VMEM] * 4, VMEM, work // total)(
        incoming, t_high, t_low, t_parts
    )

    def all_kernel(in_ref, high_ref, low_ref, part_ref, out_ref):
        for n in range(half):
            for e in range(total):
                out_ref[n, e] = part_ref[n, e] + rows(in_ref[n], high_ref[n, e], low_ref[n, e])

    backs = call(all_kernel, field, [VMEM] * 4, VMEM, work)(
        incoming, t_high, t_low, t_parts
    )
    y_high, y_low = composed(mine_q, got_q, list(range(total))[::-1], 2 * heavy)

    incoming = jnp.zeros_like(outgoing)
    for k in reversed(range(1, chips)):
        got = lax.ppermute(outgoing, "axial", [(2 * k + c, 2 * k - 2 + c) for c in range(2)])
        incoming = incoming + got
        if k > 1:
            outgoing = call(hop_kernel(0), edge, [VMEM] * 4, VMEM, work // total)(
                got, y_high, y_low, backs
            )

    def last_kernel(in_ref, high_ref, low_ref, part_ref, mine_ref, other_ref, all_ref):
        for n in range(half):
            for e in range(total):
                all_ref[n, e] = part_ref[n, e] + rows(in_ref[n], high_ref[n, e], low_ref[n, e])
        first = core_index() * elems
        away = (1 - core_index()) * elems
        for n in range(half):
            for e in range(elems):
                mine_ref[n, e] = all_ref[n, first + e]
                other_ref[n, e] = all_ref[n, away + e]

    part = struct(half, elems, vecs, size)
    mine_z, other_z = call(
        last_kernel,
        (part, part),
        [VMEM] * 4,
        (VMEM,) * 2,
        work,
        scratch_shapes=[pltpu.VMEM(field.shape, F32)],
    )(incoming, y_high, y_low, backs)
    got_z = lax.ppermute(other_z, "axial", partner)

    face = proj_table.shape[1]
    wide = -(-face // 128) * 128
    groups = lax.axis_size("theta")
    crossings = intersection_list.shape[1]

    def trace_kernel(mine_ref, got_ref, out_ref, rows_ref):
        core = core_index()
        rows_ref[...] = jnp.zeros_like(rows_ref)
        for source, base in ((mine_ref, core * half), (got_ref, (1 - core) * half)):
            for n in range(half):
                at = pl.multiple_of((base + n) * vecs, vecs)
                rows_ref[pl.ds(at, vecs), :face] = source[n, elems - 1, :, size - face :]
        out_ref[...] = rows_ref[...].T[:face]

    traces = call(
        trace_kernel,
        struct(face, lines * vecs),
        [VMEM] * 2,
        VMEM,
        scratch_shapes=[pltpu.VMEM((lines * vecs, wide), F32)],
    )(mine_z, got_z)
    blocks = [traces]
    for s in range(1, groups):
        ring = [(t, t ^ s) for t in range(groups)]
        blocks.append(lax.ppermute(traces, "theta", ring))

    def join_kernel(mine_ref, got_ref, field_ref):
        core = core_index()
        for source, base in ((mine_ref, core * half), (got_ref, (1 - core) * half)):
            for n in range(half):
                field_ref[base + n] = source[n]

    solution = call(
        join_kernel, jax.ShapeDtypeStruct(rhs_field.shape, F32), [VMEM] * 2, VMEM
    )(mine_z, got_z)

    def mortar_kernel(list_ref, index_ref, angle_ref, table_ref, *rest):
        *block_refs, out_ref, rows_ref = rest
        here = lax.axis_index("theta")
        for s in range(groups):
            block = block_refs[s][...]
            if wide > face:
                block = jnp.concatenate(
                    [block, jnp.zeros((wide - face, lines * vecs), F32)], axis=0
                )
            rows_ref[s] = block.T
        for g in range(lines):
            sums = jnp.zeros((vecs, face), F32)
            for k in range(crossings):
                face_id = lax.rem(list_ref[g, k] + angle_ref[0], lines * groups)
                shift = lax.bitwise_xor(here, lax.div(face_id, lines))
                at = pl.multiple_of(lax.rem(face_id, lines) * vecs, vecs)
                trace = rows_ref[shift, pl.ds(at, vecs), :face]
                sums = sums + dot3(split(trace), split(table_ref[index_ref[g, k]]), RIGHT_T)
            out_ref[g] = sums

    mortar = call(
        mortar_kernel,
        jax.ShapeDtypeStruct((lines, vecs, face), F32),
        [SMEM] * 3 + [VMEM] * (1 + groups),
        VMEM,
        scratch_shapes=[pltpu.VMEM((groups, lines * vecs, wide), F32)],
    )(intersection_list, proj_index, angle_step, proj_table, *blocks)
    return (solution, mortar.reshape(1, lines, vecs * face))


def solution(mesh):
    block = P("theta", "axial", None, None)
    return jax.shard_map(
        local,
        mesh=mesh,
        in_specs=(block, block, block, block, P(), P("theta", None), P("theta", None), P()),
        out_specs=(block, P("axial", "theta", None)),
        check_vma=False,
    )
```

time: 73 us -> 75.4 us (1.033)
  waiting for transfers between devices: 28.2 us -> 30.4 us
    ppermute x3, waiting for transfers between devices: 0.01 us -> 2.33 us  [local(): lax.ppermute(outgoing, 'axial', [(2 * k + c, 2 * k + 2 + c) for c in rang...]
    ppermute x1, waiting for transfers between devices: 0.01 us -> 1.08 us  [local(): got_p = lax.ppermute(other_p, 'axial', partner)]
    pallas_call x1, Pallas kernels: 5.71 us -> 4.73 us  [first_products(): call(kernel, [struct(*shape) for shape in (matrix, column, matrix, matrix...]
    ppermute x3, waiting for transfers between devices: 4.91 us -> 3.95 us  [local(): blocks.append(lax.ppermute(traces, 'theta', ring))]
    pallas_call x7 -> x8, Pallas kernels: 14.9 us -> 15.5 us  [the longest x2 6.71 us: composed(): call(kernel, shapes, specs, [VMEM] * len(shapes), flops, scratch_shapes=s...]
  transfers between devices with their start and end apart: 13 -> 13, of which waited for: 5 -> 7; matrix products, arithmetic and copies ran while one was open for 0% -> 0% of each run, Pallas kernels for 23% -> 13%
where the time goes in v1:
time: 75.4 us; the launch traced here: 75.2 us
  waiting for transfers between devices  30.4 us (40%)
  Pallas kernels  27.7 us (37%)
  starting transfers between devices  14.6 us (19%)
  between operations  1.52 us (2%)
  local copies, waits for them, and re-layouts  0.96 us (1%)
    ppermute x3, waiting for transfers between devices, local(): lax.ppermute(outgoing, 'axial', [(2 * k + c, 2 * k - 2 + c) for c in rang...  17.9 us
    pallas_call x2, Pallas kernels, composed(): call(kernel, shapes, specs, [VMEM] * len(shapes), flops, scratch_shapes=s...  6.71 us
    ppermute x3, starting transfers between devices, local(): lax.ppermute(outgoing, 'axial', [(2 * k + c, 2 * k + 2 + c) for c in rang...  6.27 us
    pallas_call x1, Pallas kernels, first_products(): call(kernel, [struct(*shape) for shape in (matrix, column, matrix, matrix...  4.73 us
    ppermute x3, starting transfers between devices, local(): blocks.append(lax.ppermute(traces, 'theta', ring))  4.45 us
    ppermute x3, waiting for transfers between devices, local(): blocks.append(lax.ppermute(traces, 'theta', ring))  3.95 us
    pallas_call x2, Pallas kernels, late_products(): call(kernel, struct(*left.shape), [VMEM] * 2, VMEM, flops, scratch_shapes...  3.92 us
    ppermute x1, waiting for transfers between devices, local(): got_g = lax.ppermute(other_g, 'axial', partner)  3.74 us
  transfers between devices with their start and end apart: 13, of which 7 were waited for; matrix products, arithmetic and copies ran while one was open for 0% of the time, Pallas kernels for 13%

profile of v1, /device:TPU:0, one launch (start us, length us, event | category | flops | bytes accessed | tf_op | source)
XLA Modules:
  0.0 75.2 jit_solution(10243800065069966154)
XLA Ops:
  0.6 4.7 %shard_map.95 = (f32[2,2,320,320]{3,2,1,0:T(8,128)S(1)}, f32[2,2,32,320]{3,2,1,0:T(8,128)S(1)}, f32[2,2,320,320]{3,2,1,0:T(8,128)S(1)}, f32[2,2,320,320]{3,2,1,0...) custom-call(f32[4,2,320,320]{3,2,1,0:T(8,128)} %left_hbm.1, f32[4,2,320,320]{3,2,1,0:T(8,128)} %right_hbm.1, ...), custom_call_target="tpu_custom_call" | custom-call | flops 786432000 | tf_op jit(solution)/shard_map/pallas_call | solution.py:119
  5.4 0.6 collective-permute-start
  5.9 2.5 %shard_map.96 = (f32[2,2,320,320]{3,2,1,0:T(8,128)S(1)}, f32[2,2,32,320]{3,2,1,0:T(8,128)S(1)}) custom-call(f32[2,2,320,320]{3,2,1,0:T(8,128)S(1)} %get-tuple-element.21.left_ref, f32[2,2,320,320]{3,2,1,0:T(8,128)S(1)} %get-tuple-element.22.right_ref, f32[2,2,32,320]{3,2,1,0:T(8,128)S(1)} %get-tuple-element.23.rhs_ref), custom_call_target="tpu_custom_call" | custom-call | flops 786432000 | tf_op jit(solution)/shard_map/pallas_call | solution.py:136
  8.5 1.1 %collective-permute-done.got_ref = f32[2,2,320,320]{3,2,1,0:T(8,128)S(1)} collective-permute-done((f32[2,2,320,320]{3,2,1,0:T(8,128)S(1)}, f32[2,2,320,320]{3,2,1,0:T(8,128)S(1)}, u32[]{:S(2)}, u32[]{:S(2)}) %collective-permute-start) | collective-permute-done | bytes 1638432 | tf_op jit(solution)/shard_map/ppermute | solution.py:290
  9.5 3.8 %shard_map.98 = (bf16[2,4,320,320]{3,2,1,0:T(8,128)(2,1)S(1)}, bf16[2,4,320,320]{3,2,1,0:T(8,128)(2,1)S(1)}, f32[2,2,320,320]{3,2,1,0:T(8,128)S(1)}, f32[2,2,320,320]{3,2,1,0:T(8,128)S(1)}) custom-call(f32[2,2,320,320]{3,2,1,0:T(8,128)S(1)} %get-tuple-element.24.mine_ref, f32[2,2,320,320]{3,2,1,0:T(8,128)S(1)} %collective-permute-done.got_ref, ...), custom_call_target="tpu_custom_call" | custom-call | flops 1572864000 | tf_op jit(solution)/shard_map/pallas_call | solution.py:214
  13.3 2.0 %shard_map.102 = f32[2,2,320,320]{3,2,1,0:T(8,128)S(1)} custom-call(f32[2,2,320,320]{3,2,1,0:T(8,128)S(1)} %get-tuple-element.31.left_ref, f32[2,2,320,320]{3,2,1,0:T(8,128)S(1)} %get-tuple-element.32.right_ref), custom_call_target="tpu_custom_call" | custom-call | flops 786432000 | tf_op jit(solution)/shard_map/pallas_call | solution.py:157
  15.3 0.4 collective-permute-start.5
  15.7 0.1 collective-permute-start.1
  15.9 3.7 %collective-permute-done.1.got_g_ref = f32[2,2,32,320]{3,2,1,0:T(8,128)S(1)} collective-permute-done((f32[2,2,32,320]{3,2,1,0:T(8,128)S(1)}, f32[2,2,32,320]{3,2,1,0:T(8,128)S(1)}, u32[]{:S(2)}, u32[]{:S(2)}) %collective-permute-start.1) | collective-permute-done | bytes 163872 | tf_op jit(solution)/shard_map/ppermute | solution.py:291
  19.6 1.1 %shard_map.97.part_ref = f32[2,4,32,320]{3,2,1,0:T(8,128)S(1)} custom-call(f32[2,2,320,320]{3,2,1,0:T(8,128)S(1)} %get-tuple-element.24.mine_ref, f32[2,2,320,320]{3,2,1,0:T(8,128)S(1)} %collective-permute-done.got_ref, f32[2,2,32,320]{3,2,1,0:T(8,128)S(1)} %get-tuple-element.26.mine_g_ref, f32[2,2,32,320]{3,2,1,0:T(8,128)S(1)} %collective-permute-done.1.got_g_ref), custom_call_target="tpu_custom_call" | custom-call | flops 157286400 | tf_op jit(solution)/shard_map/pallas_call | solution.py:303
  20.7 4.8 %collective-permute-start.2 = (f32[2,32,320]{2,1,0:T(8,128)S(1)}, f32[2,32,320]{2,1,0:T(8,128)S(1)}, u32[]{:S(2)}, u32[]{:S(2)}) collective-permute-start(f32[2,32,320]{2,1,0:T(8,128)S(1)} %slice_bitcast_fusion), channel_id=1, source_target_pairs={{0,8},{4,12},{1,9},{5,13},{2,10},{6,14},{3,11},{7,15}} | collective-permute-start | bytes 245768 | tf_op jit(solution)/shard_map/ppermute | solution.py:321
  25.5 2.3 %collective-permute-done.2.in_ref = f32[2,32,320]{2,1,0:T(8,128)S(1)} collective-permute-done((f32[2,32,320]{2,1,0:T(8,128)S(1)}, f32[2,32,320]{2,1,0:T(8,128)S(1)}, u32[]{:S(2)}, u32[]{:S(2)}) %collective-permute-start.2) | collective-permute-done | bytes 81952 | tf_op jit(solution)/shard_map/ppermute | solution.py:321
  27.8 0.3 shard_map.99
  28.2 0.7 collective-permute-start.3
  28.8 0.0 collective-permute-done.3.in_ref
  28.8 0.3 shard_map.100
  29.1 0.8 %collective-permute-start.4 = (f32[2,32,320]{2,1,0:T(8,128)S(1)}, f32[2,32,320]{2,1,0:T(8,128)S(1)}, u32[]{:S(2)}, u32[]{:S(2)}) collective-permute-start(f32[2,32,320]{2,1,0:T(8,128)S(1)} %shard_map.100), channel_id=1, source_target_pairs={{16,24},{20,28},{17,25},{21,29},{18,26},{22,30},{19,27},{23,31}} | collective-permute-start | bytes 245768 | tf_op jit(solution)/shard_map/ppermute | solution.py:321
  30.0 2.0 %shard_map.101.mine_ref = f32[2,2,320,320]{3,2,1,0:T(8,128)S(1)} custom-call(f32[2,2,320,320]{3,2,1,0:T(8,128)S(1)} %get-tuple-element.21.left_ref, f32[2,2,320,320]{3,2,1,0:T(8,128)S(1)} %get-tuple-element.30.right_ref), custom_call_target="tpu_custom_call" | custom-call | flops 786432000 | tf_op jit(solution)/shard_map/pallas_call | solution.py:157
  32.0 0.0 collective-permute-done.5.got_ref
  32.0 3.3 %shard_map.103 = (bf16[2,4,320,320]{3,2,1,0:T(8,128)(2,1)S(1)}, bf16[2,4,320,320]{3,2,1,0:T(8,128)(2,1)S(1)}, f32[2,4,32,320]{3,2,1,0:T(8,128)S(1)}) custom-call(bf16[2,4,320,320]{3,2,1,0:T(8,128)(2,1)S(1)} %get-tuple-element.28.high_ref.xh_ref, bf16[2,4,320,320]{3,2,1,0:T(8,128)(2,1)S(1)} %get-tuple-element.29.low_ref.xl_ref, ...), custom_call_target="tpu_custom_call" | custom-call | flops 1572864000 | tf_op jit(solution)/shard_map/pallas_call | solution.py:243
  35.4 0.9 %shard_map.106.part_ref = f32[2,4,32,320]{3,2,1,0:T(8,128)S(1)} custom-call(f32[2,32,320]{2,1,0:T(8,128)S(1)} %add_add_fusion.1.in_ref, bf16[2,4,320,320]{3,2,1,0:T(8,128)(2,1)S(1)} %get-tuple-element.33.high_ref, bf16[2,4,320,320]{3,2,1,0:T(8,128)(2,1)S(1)} %get-tuple-element.34.low_ref, f32[2,4,32,320]{3,2,1,0:T(8,128)S(1)} %get-tuple-element.35.part_ref), custom_call_target="tpu_custom_call" | custom-call | flops 157286400 | tf_op jit(solution)/shard_map/pallas_call | solution.py:343
  36.2 0.3 shard_map.104
  36.6 0.7 collective-permute-start.6
  37.2 2.9 %shard_map.105 = (bf16[2,4,320,320]{3,2,1,0:T(8,128)(2,1)S(1)}, bf16[2,4,320,320]{3,2,1,0:T(8,128)(2,1)S(1)}) custom-call(f32[2,2,320,320]{3,2,1,0:T(8,128)S(1)} %shard_map.101.mine_ref, f32[2,2,320,320]{3,2,1,0:T(8,128)S(1)} %collective-permute-done.5.got_ref), custom_call_target="tpu_custom_call" | custom-call | flops 1572864000 | tf_op jit(solution)/shard_map/pallas_call | solution.py:214
  40.2 0.0 collective-permute-done.6.in_ref
  40.2 0.3 shard_map.107
  40.5 0.7 collective-permute-start.7
  41.2 0.0 collective-permute-done.7.in_ref
  41.2 0.3 shard_map.108
  41.5 1.3 %collective-permute-start.8 = (f32[2,32,320]{2,1,0:T(8,128)S(1)}, f32[2,32,320]{2,1,0:T(8,128)S(1)}, u32[]{:S(2)}, u32[]{:S(2)}) collective-permute-start(f32[2,32,320]{2,1,0:T(8,128)S(1)} %shard_map.108), channel_id=1, source_target_pairs={{8,0},{12,4},{9,1},{13,5},{10,2},{14,6},{11,3},{15,7}} | collective-permute-start | bytes 245768 | tf_op jit(solution)/shard_map/ppermute | solution.py:350
  42.8 17.9 %collective-permute-done.8 = f32[2,32,320]{2,1,0:T(8,128)S(1)} collective-permute-done((f32[2,32,320]{2,1,0:T(8,128)S(1)}, f32[2,32,320]{2,1,0:T(8,128)S(1)}, u32[]{:S(2)}, u32[]{:S(2)}) %collective-permute-start.8) | collective-permute-done | bytes 81952 | tf_op jit(solution)/shard_map/ppermute | solution.py:350
  60.7 0.0 copy-start.1
  60.7 0.0 copy-start.2
  60.7 0.0 copy-start
  60.7 0.9 %shard_map.109 = (f32[2,2,32,320]{3,2,1,0:T(8,128)S(1)}, f32[2,2,32,320]{3,2,1,0:T(8,128)S(1)}) custom-call(f32[2,32,320]{2,1,0:T(8,128)S(1)} %add_add_fusion.in_ref, bf16[2,4,320,320]{3,2,1,0:T(8,128)(2,1)S(1)} %get-tuple-element.36.high_ref, bf16[2,4,320,320]{3,2,1,0:T(8,128)(2,1)S(1)} %get-tuple-element.37.low_ref, f32[2,4,32,320]{3,2,1,0:T(8,128)S(1)} %shard_map.106.part_ref), custom_call_target="tpu_custom_call" | custom-call | flops 157286400 | tf_op jit(solution)/shard_map/pallas_call | solution.py:369
  61.7 0.1 collective-permute-start.9
  61.7 1.4 %collective-permute-done.9.got_ref = f32[2,2,32,320]{3,2,1,0:T(8,128)S(1)} collective-permute-done((f32[2,2,32,320]{3,2,1,0:T(8,128)S(1)}, f32[2,2,32,320]{3,2,1,0:T(8,128)S(1)}, u32[]{:S(2)}, u32[]{:S(2)}) %collective-permute-start.9) | collective-permute-done | bytes 163872 | tf_op jit(solution)/shard_map/ppermute | solution.py:377
  63.2 0.2 shard_map.111.rest_0_
  63.3 1.6 %collective-permute-start.10 = (f32[80,128]{1,0:T(8,128)S(1)}, f32[80,128]{1,0:T(8,128)S(1)}, u32[]{:S(2)}, u32[]{:S(2)}) collective-permute-start(f32[80,128]{1,0:T(8,128)S(1)} %shard_map.111.rest_0_), channel_id=1, source_target_pairs={{0,1},{1,0},{2,3},{3,2},{4,5},{5,4},{6,7},{7,6},{8,9},{9,8},{10,11... | collective-permute-start | bytes 122888 | tf_op jit(solution)/shard_map/ppermute | solution.py:403
  65.0 2.6 %collective-permute-start.11 = (f32[80,128]{1,0:T(8,128)S(1)}, f32[80,128]{1,0:T(8,128)S(1)}, u32[]{:S(2)}, u32[]{:S(2)}) collective-permute-start(f32[80,128]{1,0:T(8,128)S(1)} %shard_map.111.rest_0_), channel_id=1, source_target_pairs={{0,2},{1,3},{2,0},{3,1},{4,6},{5,7},{6,4},{7,5},{8,10},{9,11},{10,... | collective-permute-start | bytes 122888 | tf_op jit(solution)/shard_map/ppermute | solution.py:403
  67.6 0.2 collective-permute-start.12
  67.8 0.1 copy.11.list_ref
  67.9 0.1 copy.12.index_ref
  68.6 0.8 %shard_map.110 = f32[4,2,32,320]{3,2,1,0:T(8,128)} custom-call(f32[2,2,32,320]{3,2,1,0:T(8,128)S(1)} %get-tuple-element.38.mine_ref, f32[2,2,32,320]{3,2,1,0:T(8,128)S(1)} %collective-permute-done.9.got_ref), custom_call_target="tpu_custom_call" | custom-call | tf_op jit(solution)/shard_map/pallas_call | solution.py:411
  69.4 1.3 %collective-permute-done.11.rest_2_ = f32[80,128]{1,0:T(8,128)S(1)} collective-permute-done((f32[80,128]{1,0:T(8,128)S(1)}, f32[80,128]{1,0:T(8,128)S(1)}, u32[]{:S(2)}, u32[]{:S(2)}) %collective-permute-start.11) | collective-permute-done | bytes 40992 | tf_op jit(solution)/shard_map/ppermute | solution.py:403
  70.7 2.7 %collective-permute-done.12.rest_3_ = f32[80,128]{1,0:T(8,128)S(1)} collective-permute-done((f32[80,128]{1,0:T(8,128)S(1)}, f32[80,128]{1,0:T(8,128)S(1)}, u32[]{:S(2)}, u32[]{:S(2)}) %collective-permute-start.12) | collective-permute-done | bytes 40992 | tf_op jit(solution)/shard_map/ppermute | solution.py:403
  73.4 1.1 %shard_map.112 = f32[4,32,80]{2,1,0:T(8,128)S(1)} custom-call(s32[4,2]{1,0:T(4,128)S(1)} %copy.11.list_ref, s32[4,2]{1,0:T(4,128)S(1)} %copy.12.index_ref, s32[1]{0:T(128)S(6)} %copy.14.angle_ref, f32[16,80,80]{2,1,0:T(8,128)S(1)} %copy-done, f32[80,128]{1,0:T(8,128)S(1)} %shard_map.111.rest_0_, f32[80,128]{1,0:T(8,128)S(1)} %collective-permute-done.10.rest_1_, ...), custom_call_target="tpu_custom_call" | custom-call | tf_op jit(solution)/shard_map/pallas_call | solution.py:435
  74.4 0.7 reshape.7
  (8 shorter events, 0.1 us)
Async XLA Ops:
  5.4 4.2 %collective-permute-start = (f32[2,2,320,320]{3,2,1,0:T(8,128)S(1)}, f32[2,2,320,320]{3,2,1,0:T(8,128)S(1)}, u32[]{:S(2)}, u32[]{:S(2)}) collective-permute-start(f32[2,2,320,320]{3,2,1,0:T(8,128)S(1)} %get-tuple-element.25), channel_id=1, source_target_pairs={{0,4},{4,0},{8,12},{12,8},{16,20},{20,16},{24,28},{28,24},{1,5},{5... | collective-permute-start | bytes 4915208 | tf_op jit(solution)/shard_map/ppermute | solution.py:290
  15.3 16.7 %collective-permute-start.5 = (f32[2,2,320,320]{3,2,1,0:T(8,128)S(1)}, f32[2,2,320,320]{3,2,1,0:T(8,128)S(1)}, u32[]{:S(2)}, u32[]{:S(2)}) collective-permute-start(f32[2,2,320,320]{3,2,1,0:T(8,128)S(1)} %shard_map.102), channel_id=1, source_target_pairs={{0,4},{4,0},{8,12},{12,8},{16,20},{20,16},{24,28},{28,24},{1,5},{5... | collective-permute-start | bytes 4915208 | tf_op jit(solution)/shard_map/ppermute | solution.py:329
  15.7 3.9 %collective-permute-start.1 = (f32[2,2,32,320]{3,2,1,0:T(8,128)S(1)}, f32[2,2,32,320]{3,2,1,0:T(8,128)S(1)}, u32[]{:S(2)}, u32[]{:S(2)}) collective-permute-start(f32[2,2,32,320]{3,2,1,0:T(8,128)S(1)} %get-tuple-element.27), channel_id=1, source_target_pairs={{0,4},{4,0},{8,12},{12,8},{16,20},{20,16},{24,28},{28,24},{1,5},{5... | collective-permute-start | bytes 491528 | tf_op jit(solution)/shard_map/ppermute | solution.py:291
  20.7 7.1 %collective-permute-start.2 = (f32[2,32,320]{2,1,0:T(8,128)S(1)}, f32[2,32,320]{2,1,0:T(8,128)S(1)}, u32[]{:S(2)}, u32[]{:S(2)}) collective-permute-start(f32[2,32,320]{2,1,0:T(8,128)S(1)} %slice_bitcast_fusion), channel_id=1, source_target_pairs={{0,8},{4,12},{1,9},{5,13},{2,10},{6,14},{3,11},{7,15}} | collective-permute-start | bytes 245768 | tf_op jit(solution)/shard_map/ppermute | solution.py:321
  28.2 0.7 collective-permute-start.3
  29.1 2.8 %collective-permute-start.4 = (f32[2,32,320]{2,1,0:T(8,128)S(1)}, f32[2,32,320]{2,1,0:T(8,128)S(1)}, u32[]{:S(2)}, u32[]{:S(2)}) collective-permute-start(f32[2,32,320]{2,1,0:T(8,128)S(1)} %shard_map.100), channel_id=1, source_target_pairs={{16,24},{20,28},{17,25},{21,29},{18,26},{22,30},{19,27},{23,31}} | collective-permute-start | bytes 245768 | tf_op jit(solution)/shard_map/ppermute | solution.py:321
  36.6 3.6 %collective-permute-start.6 = (f32[2,32,320]{2,1,0:T(8,128)S(1)}, f32[2,32,320]{2,1,0:T(8,128)S(1)}, u32[]{:S(2)}, u32[]{:S(2)}) collective-permute-start(f32[2,32,320]{2,1,0:T(8,128)S(1)} %shard_map.104), channel_id=1, source_target_pairs={{24,16},{28,20},{25,17},{29,21},{26,18},{30,22},{27,19},{31,23}} | collective-permute-start | bytes 245768 | tf_op jit(solution)/shard_map/ppermute | solution.py:350
  40.5 0.7 collective-permute-start.7
  41.5 19.2 %collective-permute-start.8 = (f32[2,32,320]{2,1,0:T(8,128)S(1)}, f32[2,32,320]{2,1,0:T(8,128)S(1)}, u32[]{:S(2)}, u32[]{:S(2)}) collective-permute-start(f32[2,32,320]{2,1,0:T(8,128)S(1)} %shard_map.108), channel_id=1, source_target_pairs={{8,0},{12,4},{9,1},{13,5},{10,2},{14,6},{11,3},{15,7}} | collective-permute-start | bytes 245768 | tf_op jit(solution)/shard_map/ppermute | solution.py:350
  60.7 7.1 %copy-start.1 = (s32[4,2]{0,1:T(2,128)S(1)}, s32[4,2]{0,1:T(2,128)}, u32[]{:S(2)}) copy-start(s32[4,2]{0,1:T(2,128)} %param.13) | copy-start | bytes 100
  60.7 7.2 %copy-start.2 = (s32[4,2]{0,1:T(2,128)S(1)}, s32[4,2]{0,1:T(2,128)}, u32[]{:S(2)}) copy-start(s32[4,2]{0,1:T(2,128)} %param.14) | copy-start | bytes 100
  60.7 12.6 %copy-start = (f32[16,80,80]{2,1,0:T(8,128)S(1)}, f32[16,80,80]{2,1,0:T(8,128)}, u32[]{:S(2)}) copy-start(f32[16,80,80]{2,1,0:T(8,128)} %table_ref.1) | copy-start | bytes 1228804
  61.7 1.5 %collective-permute-start.9 = (f32[2,2,32,320]{3,2,1,0:T(8,128)S(1)}, f32[2,2,32,320]{3,2,1,0:T(8,128)S(1)}, u32[]{:S(2)}, u32[]{:S(2)}) collective-permute-start(f32[2,2,32,320]{3,2,1,0:T(8,128)S(1)} %get-tuple-element.39), channel_id=1, source_target_pairs={{0,4},{4,0},{8,12},{12,8},{16,20},{20,16},{24,28},{28,24},{1,5},{5... | collective-permute-start | bytes 491528 | tf_op jit(solution)/shard_map/ppermute | solution.py:377
  63.3 6.1 %collective-permute-start.10 = (f32[80,128]{1,0:T(8,128)S(1)}, f32[80,128]{1,0:T(8,128)S(1)}, u32[]{:S(2)}, u32[]{:S(2)}) collective-permute-start(f32[80,128]{1,0:T(8,128)S(1)} %shard_map.111.rest_0_), channel_id=1, source_target_pairs={{0,1},{1,0},{2,3},{3,2},{4,5},{5,4},{6,7},{7,6},{8,9},{9,8},{10,11... | collective-permute-start | bytes 122888 | tf_op jit(solution)/shard_map/ppermute | solution.py:403
  65.0 5.7 %collective-permute-start.11 = (f32[80,128]{1,0:T(8,128)S(1)}, f32[80,128]{1,0:T(8,128)S(1)}, u32[]{:S(2)}, u32[]{:S(2)}) collective-permute-start(f32[80,128]{1,0:T(8,128)S(1)} %shard_map.111.rest_0_), channel_id=1, source_target_pairs={{0,2},{1,3},{2,0},{3,1},{4,6},{5,7},{6,4},{7,5},{8,10},{9,11},{10,... | collective-permute-start | bytes 122888 | tf_op jit(solution)/shard_map/ppermute | solution.py:403
  67.6 5.8 %collective-permute-start.12 = (f32[80,128]{1,0:T(8,128)S(1)}, f32[80,128]{1,0:T(8,128)S(1)}, u32[]{:S(2)}, u32[]{:S(2)}) collective-permute-start(f32[80,128]{1,0:T(8,128)S(1)} %shard_map.111.rest_0_), channel_id=1, source_target_pairs={{0,3},{1,2},{2,1},{3,0},{4,7},{5,6},{6,5},{7,4},{8,11},{9,10},{10,... | collective-permute-start | bytes 122888 | tf_op jit(solution)/shard_map/ppermute | solution.py:403

commit v2 on v1

--- a/solution.py
+++ b/solution.py
@@ -225,19 +225,22 @@
         out_high, out_low, out_part, left_stage, right_stage,
     ):
         last = total - 1
-        for n in range(half):
-            out_high[n, last] = xh_ref[n, last]
-            out_low[n, last] = xl_ref[n, last]
-            out_part[n, last] = part_ref[n, last]
-        for e in reversed(range(last)):
+
+        @pl.when(lax.axis_index("axial") >= lax.axis_size("axial") - 2)
+        def _():
             for n in range(half):
-                stage_left(left_stage, n, 0, size, out_high[n, e + 1], out_low[n, e + 1])
-                stage_left(left_stage, n, size, vecs, *split(out_part[n, e + 1]))
-                stage_right(right_stage, n, *split(pick(mine_ref, got_ref, n, e)))
-                result = dot(left_stage[n], right_stage[n])
-                x = xh_ref[n, e].astype(F32) + xl_ref[n, e].astype(F32)
-                out_high[n, e], out_low[n, e] = split(x + result[:size])
-                out_part[n, e] = part_ref[n, e] + result[size:]
+                out_high[n, last] = xh_ref[n, last]
+                out_low[n, last] = xl_ref[n, last]
+                out_part[n, last] = part_ref[n, last]
+            for e in reversed(range(last)):
+                for n in range(half):
+                    stage_left(left_stage, n, 0, size, out_high[n, e + 1], out_low[n, e + 1])
+                    stage_left(left_stage, n, size, vecs, *split(out_part[n, e + 1]))
+                    stage_right(right_stage, n, *split(pick(mine_ref, got_ref, n, e)))
+                    result = dot(left_stage[n], right_stage[n])
+                    x = xh_ref[n, e].astype(F32) + xl_ref[n, e].astype(F32)
+                    out_high[n, e], out_low[n, e] = split(x + result[:size])
+                    out_part[n, e] = part_ref[n, e] + result[size:]
 
     shape = struct(*x_high.shape, dtype=BF16)
     return call(
@@ -331,17 +334,28 @@
 
     t_high, t_low, t_parts = turned(x_high, x_low, parts, mine_q, got_q, 2 * heavy)
 
-    outgoing = call(hop_kernel(0), edge, [VMEM] * 4, VMEM, work // total)(
+    def turn_kernel(*refs):
+        @pl.when(lax.axis_index("axial") >= devices - 2)
+        def _():
+            hop_kernel(0)(*refs)
+
+    outgoing = call(turn_kernel, edge, [VMEM] * 4, VMEM, work // total)(
         incoming, t_high, t_low, t_parts
     )
 
-    def all_kernel(in_ref, high_ref, low_ref, part_ref, out_ref):
+    def back_kernel(in_ref, high_ref, low_ref, part_ref, mine_ref, got_ref, out_ref):
         for n in range(half):
             for e in range(total):
                 out_ref[n, e] = part_ref[n, e] + rows(in_ref[n], high_ref[n, e], low_ref[n, e])
-
-    backs = call(all_kernel, field, [VMEM] * 4, VMEM, work)(
-        incoming, t_high, t_low, t_parts
+        for n in range(half):
+            current = out_ref[n, total - 1]
+            for e in reversed(range(total - 1)):
+                operator = split(pick(mine_ref, got_ref, n, e))
+                current = out_ref[n, e] + rows(current, *operator)
+                out_ref[n, e] = current
+
+    backs = call(back_kernel, field, [VMEM] * 6, VMEM, 2 * work)(
+        incoming, x_high, x_low, parts, mine_q, got_q
     )
     y_high, y_low = composed(mine_q, got_q, list(range(total))[::-1], 2 * heavy)
 

time: 75.4 us -> 74.3 us (0.985)
  Pallas kernels: 27.7 us -> 25 us
  waiting for transfers between devices: 30.4 us -> 32 us
    pallas_call x1, Pallas kernels: 3.35 us -> 0.02 us  [turned(): call(kernel, [shape, shape, struct(*parts.shape)], [VMEM] * 5, [VMEM] * 3...]
    ppermute x3, waiting for transfers between devices: 17.9 us -> 19.5 us  [local(): lax.ppermute(outgoing, 'axial', [(2 * k + c, 2 * k - 2 + c) for c in rang...]
    pallas_call x1 -> x2, Pallas kernels: 0.87 us -> 1.86 us  [the longest x1 1.84 us: local(): call(back_kernel, field, [VMEM] * 6, VMEM, 2 * work)]
  transfers between devices with their start and end apart: 13 -> 13, of which waited for: 7 -> 7; matrix products, arithmetic and copies ran while one was open for 0% -> 0% of each run, Pallas kernels for 13% -> 16%
where the time goes in v2:
time: 74.3 us; the launch traced here: 74.1 us
  waiting for transfers between devices  32 us (43%)
  Pallas kernels  25 us (34%)
  starting transfers between devices  14.6 us (20%)
  between operations  1.53 us (2%)
  local copies, waits for them, and re-layouts  0.96 us (1%)
    ppermute x3, waiting for transfers between devices, local(): lax.ppermute(outgoing, 'axial', [(2 * k + c, 2 * k - 2 + c) for c in rang...  19.5 us
    pallas_call x2, Pallas kernels, composed(): call(kernel, shapes, specs, [VMEM] * len(shapes), flops, scratch_shapes=s...  6.72 us
    ppermute x3, starting transfers between devices, local(): lax.ppermute(outgoing, 'axial', [(2 * k + c, 2 * k + 2 + c) for c in rang...  6.27 us
    pallas_call x1, Pallas kernels, first_products(): call(kernel, [struct(*shape) for shape in (matrix, column, matrix, matrix...  4.73 us
    ppermute x3, starting transfers between devices, local(): blocks.append(lax.ppermute(traces, 'theta', ring))  4.45 us
    ppermute x3, waiting for transfers between devices, local(): blocks.append(lax.ppermute(traces, 'theta', ring))  3.95 us
    pallas_call x2, Pallas kernels, late_products(): call(kernel, struct(*left.shape), [VMEM] * 2, VMEM, flops, scratch_shapes...  3.92 us
    ppermute x1, waiting for transfers between devices, local(): got_g = lax.ppermute(other_g, 'axial', partner)  3.74 us
  transfers between devices with their start and end apart: 13, of which 7 were waited for; matrix products, arithmetic and copies ran while one was open for 0% of the time, Pallas kernels for 16%

profile of v2, /device:TPU:0, one launch (start us, length us, event | category | flops | bytes accessed | tf_op | source)
XLA Modules:
  0.0 74.1 jit_solution(2948383086636268274)
XLA Ops:
  0.6 4.7 %shard_map.95 = (f32[2,2,320,320]{3,2,1,0:T(8,128)S(1)}, f32[2,2,32,320]{3,2,1,0:T(8,128)S(1)}, f32[2,2,320,320]{3,2,1,0:T(8,128)S(1)}, f32[2,2,320,320]{3,2,1,0...) custom-call(f32[4,2,320,320]{3,2,1,0:T(8,128)} %left_hbm.1, f32[4,2,320,320]{3,2,1,0:T(8,128)} %right_hbm.1, ...), custom_call_target="tpu_custom_call" | custom-call | flops 786432000 | tf_op jit(solution)/shard_map/pallas_call | solution.py:119
  5.4 0.6 collective-permute-start
  5.9 2.5 %shard_map.96 = (f32[2,2,320,320]{3,2,1,0:T(8,128)S(1)}, f32[2,2,32,320]{3,2,1,0:T(8,128)S(1)}) custom-call(f32[2,2,320,320]{3,2,1,0:T(8,128)S(1)} %get-tuple-element.21.left_ref, f32[2,2,320,320]{3,2,1,0:T(8,128)S(1)} %get-tuple-element.22.right_ref, f32[2,2,32,320]{3,2,1,0:T(8,128)S(1)} %get-tuple-element.23.rhs_ref), custom_call_target="tpu_custom_call" | custom-call | flops 786432000 | tf_op jit(solution)/shard_map/pallas_call | solution.py:136
  8.5 1.1 %collective-permute-done.got_ref = f32[2,2,320,320]{3,2,1,0:T(8,128)S(1)} collective-permute-done((f32[2,2,320,320]{3,2,1,0:T(8,128)S(1)}, f32[2,2,320,320]{3,2,1,0:T(8,128)S(1)}, u32[]{:S(2)}, u32[]{:S(2)}) %collective-permute-start) | collective-permute-done | bytes 1638432 | tf_op jit(solution)/shard_map/ppermute | solution.py:293
  9.5 3.8 %shard_map.98 = (bf16[2,4,320,320]{3,2,1,0:T(8,128)(2,1)S(1)}, bf16[2,4,320,320]{3,2,1,0:T(8,128)(2,1)S(1)}, f32[2,2,320,320]{3,2,1,0:T(8,128)S(1)}, f32[2,2,320,320]{3,2,1,0:T(8,128)S(1)}) custom-call(f32[2,2,320,320]{3,2,1,0:T(8,128)S(1)} %get-tuple-element.24.mine_ref, f32[2,2,320,320]{3,2,1,0:T(8,128)S(1)} %collective-permute-done.got_ref, ...), custom_call_target="tpu_custom_call" | custom-call | flops 1572864000 | tf_op jit(solution)/shard_map/pallas_call | solution.py:214
  13.3 2.0 %shard_map.102 = f32[2,2,320,320]{3,2,1,0:T(8,128)S(1)} custom-call(f32[2,2,320,320]{3,2,1,0:T(8,128)S(1)} %get-tuple-element.31.left_ref, f32[2,2,320,320]{3,2,1,0:T(8,128)S(1)} %get-tuple-element.32.right_ref), custom_call_target="tpu_custom_call" | custom-call | flops 786432000 | tf_op jit(solution)/shard_map/pallas_call | solution.py:157
  15.3 0.4 collective-permute-start.5
  15.7 0.1 collective-permute-start.1
  15.9 3.7 %collective-permute-done.1.got_g_ref = f32[2,2,32,320]{3,2,1,0:T(8,128)S(1)} collective-permute-done((f32[2,2,32,320]{3,2,1,0:T(8,128)S(1)}, f32[2,2,32,320]{3,2,1,0:T(8,128)S(1)}, u32[]{:S(2)}, u32[]{:S(2)}) %collective-permute-start.1) | collective-permute-done | bytes 163872 | tf_op jit(solution)/shard_map/ppermute | solution.py:294
  19.6 1.1 %shard_map.97.part_ref = f32[2,4,32,320]{3,2,1,0:T(8,128)S(1)} custom-call(f32[2,2,320,320]{3,2,1,0:T(8,128)S(1)} %get-tuple-element.24.mine_ref, f32[2,2,320,320]{3,2,1,0:T(8,128)S(1)} %collective-permute-done.got_ref, f32[2,2,32,320]{3,2,1,0:T(8,128)S(1)} %get-tuple-element.26.mine_g_ref, f32[2,2,32,320]{3,2,1,0:T(8,128)S(1)} %collective-permute-done.1.got_g_ref), custom_call_target="tpu_custom_call" | custom-call | flops 157286400 | tf_op jit(solution)/shard_map/pallas_call | solution.py:306
  20.7 4.8 %collective-permute-start.2 = (f32[2,32,320]{2,1,0:T(8,128)S(1)}, f32[2,32,320]{2,1,0:T(8,128)S(1)}, u32[]{:S(2)}, u32[]{:S(2)}) collective-permute-start(f32[2,32,320]{2,1,0:T(8,128)S(1)} %slice_bitcast_fusion), channel_id=1, source_target_pairs={{0,8},{4,12},{1,9},{5,13},{2,10},{6,14},{3,11},{7,15}} | collective-permute-start | bytes 245768 | tf_op jit(solution)/shard_map/ppermute | solution.py:324
  25.5 2.3 %collective-permute-done.2.in_ref = f32[2,32,320]{2,1,0:T(8,128)S(1)} collective-permute-done((f32[2,32,320]{2,1,0:T(8,128)S(1)}, f32[2,32,320]{2,1,0:T(8,128)S(1)}, u32[]{:S(2)}, u32[]{:S(2)}) %collective-permute-start.2) | collective-permute-done | bytes 81952 | tf_op jit(solution)/shard_map/ppermute | solution.py:324
  27.8 0.3 shard_map.99
  28.2 0.7 collective-permute-start.3
  28.8 0.0 collective-permute-done.3.in_ref
  28.8 0.3 shard_map.100
  29.1 0.8 %collective-permute-start.4 = (f32[2,32,320]{2,1,0:T(8,128)S(1)}, f32[2,32,320]{2,1,0:T(8,128)S(1)}, u32[]{:S(2)}, u32[]{:S(2)}) collective-permute-start(f32[2,32,320]{2,1,0:T(8,128)S(1)} %shard_map.100), channel_id=1, source_target_pairs={{16,24},{20,28},{17,25},{21,29},{18,26},{22,30},{19,27},{23,31}} | collective-permute-start | bytes 245768 | tf_op jit(solution)/shard_map/ppermute | solution.py:324
  30.0 2.0 %shard_map.101.mine_ref = f32[2,2,320,320]{3,2,1,0:T(8,128)S(1)} custom-call(f32[2,2,320,320]{3,2,1,0:T(8,128)S(1)} %get-tuple-element.21.left_ref, f32[2,2,320,320]{3,2,1,0:T(8,128)S(1)} %get-tuple-element.30.right_ref), custom_call_target="tpu_custom_call" | custom-call | flops 786432000 | tf_op jit(solution)/shard_map/pallas_call | solution.py:157
  32.0 0.0 collective-permute-done.4
  32.0 0.0 collective-permute-done.5.got_ref
  32.1 0.7 collective-permute-start.6
  32.7 2.9 %shard_map.105 = (bf16[2,4,320,320]{3,2,1,0:T(8,128)(2,1)S(1)}, bf16[2,4,320,320]{3,2,1,0:T(8,128)(2,1)S(1)}) custom-call(f32[2,2,320,320]{3,2,1,0:T(8,128)S(1)} %shard_map.101.mine_ref, f32[2,2,320,320]{3,2,1,0:T(8,128)S(1)} %collective-permute-done.5.got_ref), custom_call_target="tpu_custom_call" | custom-call | flops 1572864000 | tf_op jit(solution)/shard_map/pallas_call | solution.py:214
  35.7 1.8 %shard_map.106.part_ref = f32[2,4,32,320]{3,2,1,0:T(8,128)S(1)} custom-call(f32[2,32,320]{2,1,0:T(8,128)S(1)} %add_add_fusion.1.refs_0_.in_ref, bf16[2,4,320,320]{3,2,1,0:T(8,128)(2,1)S(1)} %get-tuple-element.28.high_ref.xh_ref, bf16[2,4,320,320]{3,2,1,0:T(8,128)(2,1)S(1)} %get-tuple-element.29.low_ref.xl_ref, f32[2,4,32,320]{3,2,1,0:T(8,128)S(1)} %shard_map.97.part_ref, ...), custom_call_target="tpu_custom_call" | custom-call | flops 314572800 | tf_op jit(solution)/shard_map/pallas_call | solution.py:357
  37.5 0.0 collective-permute-done.6.in_ref
  37.5 0.3 shard_map.107
  37.9 0.7 collective-permute-start.7
  38.5 0.0 collective-permute-done.7.in_ref
  38.5 0.3 shard_map.108
  38.8 1.3 %collective-permute-start.8 = (f32[2,32,320]{2,1,0:T(8,128)S(1)}, f32[2,32,320]{2,1,0:T(8,128)S(1)}, u32[]{:S(2)}, u32[]{:S(2)}) collective-permute-start(f32[2,32,320]{2,1,0:T(8,128)S(1)} %shard_map.108), channel_id=1, source_target_pairs={{8,0},{12,4},{9,1},{13,5},{10,2},{14,6},{11,3},{15,7}} | collective-permute-start | bytes 245768 | tf_op jit(solution)/shard_map/ppermute | solution.py:364
  40.1 19.5 %collective-permute-done.8 = f32[2,32,320]{2,1,0:T(8,128)S(1)} collective-permute-done((f32[2,32,320]{2,1,0:T(8,128)S(1)}, f32[2,32,320]{2,1,0:T(8,128)S(1)}, u32[]{:S(2)}, u32[]{:S(2)}) %collective-permute-start.8) | collective-permute-done | bytes 81952 | tf_op jit(solution)/shard_map/ppermute | solution.py:364
  59.7 0.0 copy-start.1
  59.7 0.0 copy-start.2
  59.7 0.0 copy-start
  59.7 0.9 %shard_map.109 = (f32[2,2,32,320]{3,2,1,0:T(8,128)S(1)}, f32[2,2,32,320]{3,2,1,0:T(8,128)S(1)}) custom-call(f32[2,32,320]{2,1,0:T(8,128)S(1)} %add_add_fusion.in_ref, bf16[2,4,320,320]{3,2,1,0:T(8,128)(2,1)S(1)} %get-tuple-element.36.high_ref, bf16[2,4,320,320]{3,2,1,0:T(8,128)(2,1)S(1)} %get-tuple-element.37.low_ref, f32[2,4,32,320]{3,2,1,0:T(8,128)S(1)} %shard_map.106.part_ref), custom_call_target="tpu_custom_call" | custom-call | flops 157286400 | tf_op jit(solution)/shard_map/pallas_call | solution.py:383
  60.6 0.1 collective-permute-start.9
  60.7 1.4 %collective-permute-done.9.got_ref = f32[2,2,32,320]{3,2,1,0:T(8,128)S(1)} collective-permute-done((f32[2,2,32,320]{3,2,1,0:T(8,128)S(1)}, f32[2,2,32,320]{3,2,1,0:T(8,128)S(1)}, u32[]{:S(2)}, u32[]{:S(2)}) %collective-permute-start.9) | collective-permute-done | bytes 163872 | tf_op jit(solution)/shard_map/ppermute | solution.py:391
  62.1 0.2 shard_map.111.rest_0_
  62.3 1.6 %collective-permute-start.10 = (f32[80,128]{1,0:T(8,128)S(1)}, f32[80,128]{1,0:T(8,128)S(1)}, u32[]{:S(2)}, u32[]{:S(2)}) collective-permute-start(f32[80,128]{1,0:T(8,128)S(1)} %shard_map.111.rest_0_), channel_id=1, source_target_pairs={{0,1},{1,0},{2,3},{3,2},{4,5},{5,4},{6,7},{7,6},{8,9},{9,8},{10,11... | collective-permute-start | bytes 122888 | tf_op jit(solution)/shard_map/ppermute | solution.py:417
  63.9 2.6 %collective-permute-start.11 = (f32[80,128]{1,0:T(8,128)S(1)}, f32[80,128]{1,0:T(8,128)S(1)}, u32[]{:S(2)}, u32[]{:S(2)}) collective-permute-start(f32[80,128]{1,0:T(8,128)S(1)} %shard_map.111.rest_0_), channel_id=1, source_target_pairs={{0,2},{1,3},{2,0},{3,1},{4,6},{5,7},{6,4},{7,5},{8,10},{9,11},{10,... | collective-permute-start | bytes 122888 | tf_op jit(solution)/shard_map/ppermute | solution.py:417
  66.5 0.2 collective-permute-start.12
  66.7 0.1 copy.11.list_ref
  66.8 0.1 copy.12.index_ref
  67.6 0.8 %shard_map.110 = f32[4,2,32,320]{3,2,1,0:T(8,128)} custom-call(f32[2,2,32,320]{3,2,1,0:T(8,128)S(1)} %get-tuple-element.38.mine_ref, f32[2,2,32,320]{3,2,1,0:T(8,128)S(1)} %collective-permute-done.9.got_ref), custom_call_target="tpu_custom_call" | custom-call | tf_op jit(solution)/shard_map/pallas_call | solution.py:425
  68.3 0.0 collective-permute-done.10.rest_1_
  68.4 1.3 %collective-permute-done.11.rest_2_ = f32[80,128]{1,0:T(8,128)S(1)} collective-permute-done((f32[80,128]{1,0:T(8,128)S(1)}, f32[80,128]{1,0:T(8,128)S(1)}, u32[]{:S(2)}, u32[]{:S(2)}) %collective-permute-start.11) | collective-permute-done | bytes 40992 | tf_op jit(solution)/shard_map/ppermute | solution.py:417
  69.6 2.7 %collective-permute-done.12.rest_3_ = f32[80,128]{1,0:T(8,128)S(1)} collective-permute-done((f32[80,128]{1,0:T(8,128)S(1)}, f32[80,128]{1,0:T(8,128)S(1)}, u32[]{:S(2)}, u32[]{:S(2)}) %collective-permute-start.12) | collective-permute-done | bytes 40992 | tf_op jit(solution)/shard_map/ppermute | solution.py:417
  72.3 1.1 %shard_map.112 = f32[4,32,80]{2,1,0:T(8,128)S(1)} custom-call(s32[4,2]{1,0:T(4,128)S(1)} %copy.11.list_ref, s32[4,2]{1,0:T(4,128)S(1)} %copy.12.index_ref, s32[1]{0:T(128)S(6)} %copy.14.angle_ref, f32[16,80,80]{2,1,0:T(8,128)S(1)} %copy-done, f32[80,128]{1,0:T(8,128)S(1)} %shard_map.111.rest_0_, f32[80,128]{1,0:T(8,128)S(1)} %collective-permute-done.10.rest_1_, ...), custom_call_target="tpu_custom_call" | custom-call | tf_op jit(solution)/shard_map/pallas_call | solution.py:449
  73.4 0.7 %reshape.7 = f32[1,4,2560]{2,1,0:T(4,128)} reshape(f32[4,32,80]{2,1,0:T(8,128)S(1)} %shard_map.112) | data formatting | bytes 81920 | tf_op jit(solution)/shard_map/reshape | solution.py:456
  (8 shorter events, 0.1 us)
Async XLA Ops:
  5.4 4.2 %collective-permute-start = (f32[2,2,320,320]{3,2,1,0:T(8,128)S(1)}, f32[2,2,320,320]{3,2,1,0:T(8,128)S(1)}, u32[]{:S(2)}, u32[]{:S(2)}) collective-permute-start(f32[2,2,320,320]{3,2,1,0:T(8,128)S(1)} %get-tuple-element.25), channel_id=1, source_target_pairs={{0,4},{4,0},{8,12},{12,8},{16,20},{20,16},{24,28},{28,24},{1,5},{5... | collective-permute-start | bytes 4915208 | tf_op jit(solution)/shard_map/ppermute | solution.py:293
  15.3 16.7 %collective-permute-start.5 = (f32[2,2,320,320]{3,2,1,0:T(8,128)S(1)}, f32[2,2,320,320]{3,2,1,0:T(8,128)S(1)}, u32[]{:S(2)}, u32[]{:S(2)}) collective-permute-start(f32[2,2,320,320]{3,2,1,0:T(8,128)S(1)} %shard_map.102), channel_id=1, source_target_pairs={{0,4},{4,0},{8,12},{12,8},{16,20},{20,16},{24,28},{28,24},{1,5},{5... | collective-permute-start | bytes 4915208 | tf_op jit(solution)/shard_map/ppermute | solution.py:332
  15.7 3.9 %collective-permute-start.1 = (f32[2,2,32,320]{3,2,1,0:T(8,128)S(1)}, f32[2,2,32,320]{3,2,1,0:T(8,128)S(1)}, u32[]{:S(2)}, u32[]{:S(2)}) collective-permute-start(f32[2,2,32,320]{3,2,1,0:T(8,128)S(1)} %get-tuple-element.27), channel_id=1, source_target_pairs={{0,4},{4,0},{8,12},{12,8},{16,20},{20,16},{24,28},{28,24},{1,5},{5... | collective-permute-start | bytes 491528 | tf_op jit(solution)/shard_map/ppermute | solution.py:294
  20.7 7.1 %collective-permute-start.2 = (f32[2,32,320]{2,1,0:T(8,128)S(1)}, f32[2,32,320]{2,1,0:T(8,128)S(1)}, u32[]{:S(2)}, u32[]{:S(2)}) collective-permute-start(f32[2,32,320]{2,1,0:T(8,128)S(1)} %slice_bitcast_fusion), channel_id=1, source_target_pairs={{0,8},{4,12},{1,9},{5,13},{2,10},{6,14},{3,11},{7,15}} | collective-permute-start | bytes 245768 | tf_op jit(solution)/shard_map/ppermute | solution.py:324
  28.2 0.7 collective-permute-start.3
  29.1 2.8 %collective-permute-start.4 = (f32[2,32,320]{2,1,0:T(8,128)S(1)}, f32[2,32,320]{2,1,0:T(8,128)S(1)}, u32[]{:S(2)}, u32[]{:S(2)}) collective-permute-start(f32[2,32,320]{2,1,0:T(8,128)S(1)} %shard_map.100), channel_id=1, source_target_pairs={{16,24},{20,28},{17,25},{21,29},{18,26},{22,30},{19,27},{23,31}} | collective-permute-start | bytes 245768 | tf_op jit(solution)/shard_map/ppermute | solution.py:324
  32.1 5.5 %collective-permute-start.6 = (f32[2,32,320]{2,1,0:T(8,128)S(1)}, f32[2,32,320]{2,1,0:T(8,128)S(1)}, u32[]{:S(2)}, u32[]{:S(2)}) collective-permute-start(f32[2,32,320]{2,1,0:T(8,128)S(1)} %shard_map.104), channel_id=1, source_target_pairs={{24,16},{28,20},{25,17},{29,21},{26,18},{30,22},{27,19},{31,23}} | collective-permute-start | bytes 245768 | tf_op jit(solution)/shard_map/ppermute | solution.py:364
  37.9 0.7 collective-permute-start.7
  38.8 20.8 %collective-permute-start.8 = (f32[2,32,320]{2,1,0:T(8,128)S(1)}, f32[2,32,320]{2,1,0:T(8,128)S(1)}, u32[]{:S(2)}, u32[]{:S(2)}) collective-permute-start(f32[2,32,320]{2,1,0:T(8,128)S(1)} %shard_map.108), channel_id=1, source_target_pairs={{8,0},{12,4},{9,1},{13,5},{10,2},{14,6},{11,3},{15,7}} | collective-permute-start | bytes 245768 | tf_op jit(solution)/shard_map/ppermute | solution.py:364
  59.7 7.1 %copy-start.1 = (s32[4,2]{0,1:T(2,128)S(1)}, s32[4,2]{0,1:T(2,128)}, u32[]{:S(2)}) copy-start(s32[4,2]{0,1:T(2,128)} %param.13) | copy-start | bytes 100
  59.7 7.1 %copy-start.2 = (s32[4,2]{0,1:T(2,128)S(1)}, s32[4,2]{0,1:T(2,128)}, u32[]{:S(2)}) copy-start(s32[4,2]{0,1:T(2,128)} %param.14) | copy-start | bytes 100
  59.7 12.6 %copy-start = (f32[16,80,80]{2,1,0:T(8,128)S(1)}, f32[16,80,80]{2,1,0:T(8,128)}, u32[]{:S(2)}) copy-start(f32[16,80,80]{2,1,0:T(8,128)} %table_ref.1) | copy-start | bytes 1228804
  60.6 1.5 %collective-permute-start.9 = (f32[2,2,32,320]{3,2,1,0:T(8,128)S(1)}, f32[2,2,32,320]{3,2,1,0:T(8,128)S(1)}, u32[]{:S(2)}, u32[]{:S(2)}) collective-permute-start(f32[2,2,32,320]{3,2,1,0:T(8,128)S(1)} %get-tuple-element.39), channel_id=1, source_target_pairs={{0,4},{4,0},{8,12},{12,8},{16,20},{20,16},{24,28},{28,24},{1,5},{5... | collective-permute-start | bytes 491528 | tf_op jit(solution)/shard_map/ppermute | solution.py:391
  62.3 6.1 %collective-permute-start.10 = (f32[80,128]{1,0:T(8,128)S(1)}, f32[80,128]{1,0:T(8,128)S(1)}, u32[]{:S(2)}, u32[]{:S(2)}) collective-permute-start(f32[80,128]{1,0:T(8,128)S(1)} %shard_map.111.rest_0_), channel_id=1, source_target_pairs={{0,1},{1,0},{2,3},{3,2},{4,5},{5,4},{6,7},{7,6},{8,9},{9,8},{10,11... | collective-permute-start | bytes 122888 | tf_op jit(solution)/shard_map/ppermute | solution.py:417
  63.9 5.7 %collective-permute-start.11 = (f32[80,128]{1,0:T(8,128)S(1)}, f32[80,128]{1,0:T(8,128)S(1)}, u32[]{:S(2)}, u32[]{:S(2)}) collective-permute-start(f32[80,128]{1,0:T(8,128)S(1)} %shard_map.111.rest_0_), channel_id=1, source_target_pairs={{0,2},{1,3},{2,0},{3,1},{4,6},{5,7},{6,4},{7,5},{8,10},{9,11},{10,... | collective-permute-start | bytes 122888 | tf_op jit(solution)/shard_map/ppermute | solution.py:417
  66.5 5.8 %collective-permute-start.12 = (f32[80,128]{1,0:T(8,128)S(1)}, f32[80,128]{1,0:T(8,128)S(1)}, u32[]{:S(2)}, u32[]{:S(2)}) collective-permute-start(f32[80,128]{1,0:T(8,128)S(1)} %shard_map.111.rest_0_), channel_id=1, source_target_pairs={{0,3},{1,2},{2,1},{3,0},{4,7},{5,6},{6,5},{7,4},{8,11},{9,10},{10,... | collective-permute-start | bytes 122888 | tf_op jit(solution)/shard_map/ppermute | solution.py:417
